TPU v7x, 32 devices: a whole 2x2x4 slice. The times are simulated.
32 devices in a mesh: expert: 16 (over z, y, x), dp: 2 (over core).
Axes of the slice: x: 2, y: 2, z: 4, core: 2. Of those that a mesh axis runs over, the one named last changes fastest.
Arguments:
- tokens: bfloat16 [768, 2048], P(('expert', 'dp')), may hold values from -6 to 6
- cotangent: bfloat16 [768, 2048], P(('expert', 'dp')), may hold values from -6 to 6
- route_gates: bfloat16 [768, 6], P(('expert', 'dp')), may hold values from 0.049804688 to 1
- routes: int32 [768, 6], P(('expert', 'dp')), may hold values from 0 to 15, all different within a row; in each aligned block of 24 rows (0 to 23, 24 to 47, ...) at most 12 rows name the same one
- w_gate: bfloat16 [16, 1408, 2048], P('expert', 'dp'), may hold values from -0.125 to 0.125
- w_up: bfloat16 [16, 1408, 2048], P('expert', 'dp'), may hold values from -0.125 to 0.125
- w_down: bfloat16 [16, 1408, 2048], P('expert', 'dp'), may hold values from -0.15625 to 0.15625
Outputs:
- layer_out: bfloat16 [768, 2048], P(('expert', 'dp'))
- token_grad: bfloat16 [768, 2048], P(('expert', 'dp'))
- gate_grad: float32 [768, 6], P(('expert', 'dp'))
- grad_gate_proj: float32 [16, 1408, 2048], P('expert', 'dp')
- grad_up_proj: float32 [16, 1408, 2048], P('expert', 'dp')
- grad_down_proj: float32 [16, 1408, 2048], P('expert', 'dp')
Inputs may be any that keep to these rules, and one draw needn't show every extreme that they name: `routes`: each row names 6 different experts. In the rows of one device no expert is named by more than 12 rows.
All inputs are finite; a program needn't handle non-finite values.
Results may differ from a plain program's by a relative error of at most 0.01.
Values may be sent and summed in bfloat16 or wider, within the bound.
A program may use at most 128 MiB of HBM per device.

v0:
```python
import functools

import jax
import jax.numpy as jnp
from jax import lax
from jax.experimental import pallas as pl
from jax.experimental.pallas import tpu as pltpu
from jax.sharding import PartitionSpec as P

INNER = (((1,), (1,)), ((), ()))
OUTER = (((0,), (0,)), ((), ()))
LANES = 128
VMEM_LIMIT = 60 * 1024 * 1024


def dot_f32(left, right, dims=(((1,), (0,)), ((), ()))):
    return lax.dot_general(left, right, dims, preferred_element_type=jnp.float32)


class Net:
    def __init__(self, depth, group, send_sem, recv_sem):
        me, core = lax.axis_index("expert"), lax.axis_index("dp")
        z, y, x = me // 4, (me // 2) % 2, me % 2
        self.me, self.core, self.z, self.y, self.x = me, core, z, y, x

        def at(zz, yy, xx, cc):
            return (zz * 4 + yy * 2 + xx, cc)

        self.deep = [at((z + k) % depth, y, x, core) for k in range(1, depth)]
        self.across, self.beside = at(z, 1 - y, x, core), at(z, y, 1 - x, core)
        self.mates = [at(z, y, x, (core + k) % group) for k in range(1, group)]
        self.across_id, self.beside_id = self.across[0], self.beside[0]
        self.send_sem, self.recv_sem = send_sem, recv_sem
        self.sent, self.used = [], 0

    def barrier(self):
        peers = self.deep + [self.across, self.beside] + self.mates
        barrier = pltpu.get_barrier_semaphore()
        for peer in peers:
            pl.semaphore_signal(barrier, inc=1, device_id=peer, device_id_type=pl.DeviceIdType.MESH)
        pl.semaphore_wait(barrier, len(peers))

    def push(self, src, dst, peer):
        index = self.used
        self.used += 1
        copy = pltpu.make_async_remote_copy(
            src_ref=src, dst_ref=dst, send_sem=self.send_sem.at[index], recv_sem=self.recv_sem.at[index],
            device_id=peer, device_id_type=pl.DeviceIdType.MESH,
        )
        copy.start()
        self.sent.append(copy)
        return copy

    def finish(self):
        for copy in self.sent:
            copy.wait_send()


def arrived(copies):
    for copy in copies:
        copy.wait_recv()


def flat(value):
    return value.reshape(-1, value.shape[-1])


def dispatch_kernel(depth, group, top, *refs):
    (rt, tok, cot, tri, kcap), (row_rt, row_tok, row_cot, tabs) = refs[:5], refs[5:9]
    (z_rt, z_tok, z_cot, y_rt, y_tok, y_cot, x_rt, x_tok, x_cot) = refs[9:18]
    (f_rt, f0_tok, f0_cot, f1_tok, f1_cot) = refs[18:23]
    own_sem, send_sem, recv_sem = refs[23:]
    net = Net(depth, group, send_sem, recv_sem)
    z, y, x, core = net.z, net.y, net.x, net.core
    half = tok.shape[1] // 2
    low, high = pl.ds(0, half), pl.ds(half, half)
    span = row_rt.shape[3]
    net.barrier()

    own = []
    for i, (src, dst) in enumerate(((rt, z_rt), (tok, z_tok), (cot, z_cot))):
        copy = pltpu.make_async_copy(src, dst.at[z], own_sem.at[i])
        copy.start()
        own.append(copy)
    deep_rt = [net.push(rt, z_rt.at[z], peer) for peer in net.deep]
    deep_tok = [net.push(tok, z_tok.at[z], peer) for peer in net.deep]
    for copy in own:
        copy.wait()
    arrived(deep_rt)
    side_rt = [net.push(z_rt, y_rt, net.across), net.push(z_rt, x_rt, net.beside)]
    arrived(deep_tok)
    up_tok = net.push(z_tok.at[:, :, low], y_tok, net.across)
    by_tok = net.push(z_tok.at[:, :, high], x_tok, net.beside)
    deep_cot = [net.push(cot, z_cot.at[z], peer) for peer in net.deep]
    arrived(side_rt)

    lane = lax.broadcasted_iota(jnp.int32, (kcap.shape[0], LANES), 1)

    def table(which, part, source, expert, base):
        routing = flat(source[...]).astype(jnp.float32)
        named = (routing == expert.astype(jnp.float32)) & (lane < top)
        used = jnp.sum(named.astype(jnp.float32), axis=1, keepdims=True)
        used = jnp.broadcast_to(used, lane.shape)
        rank = dot_f32(tri[...], used.astype(jnp.bfloat16))
        slot = rank + kcap[...] + (base * span).astype(jnp.float32)
        hit = (used > 0.5) & (slot == lane.astype(jnp.float32))
        tabs[which, part] = hit.astype(jnp.float32).astype(jnp.bfloat16)

    table(0, 0, z_rt, net.me, y)
    table(0, 1, y_rt, net.me, 1 - y)
    table(1, 0, z_rt, net.beside_id, y)
    table(1, 1, y_rt, net.beside_id, 1 - y)
    table(2, 0, z_rt, net.me, x)
    table(2, 1, x_rt, net.me, 1 - x)
    table(3, 0, z_rt, net.across_id, x)
    table(3, 1, x_rt, net.across_id, 1 - x)

    def chosen(which, near, far):
        rows = dot_f32(tabs[which, 0], flat(near), OUTER) + dot_f32(tabs[which, 1], flat(far), OUTER)
        return rows[: 2 * span].astype(jnp.bfloat16).reshape(2, span, -1)

    def share(view):
        return [net.push(view, view, peer) for peer in net.mates]

    def first_way(near, far, send, rows, cols):
        send[...] = chosen(1, near, far)
        moved = net.push(send, rows.at[core, x, :, :, cols], net.beside)
        rows[core, x, :, :, cols] = chosen(0, near, far)
        return moved, share(rows.at[core, x, :, :, cols])

    def second_way(near, far, send, rows, cols):
        send[...] = chosen(3, near, far)
        moved = net.push(send, rows.at[core, :, y, :, cols], net.across)
        rows[core, :, y, :, cols] = chosen(2, near, far)
        return moved, share(rows.at[core, :, y, :, cols])

    pending = []
    every = pl.ds(0, LANES)
    moved_rt, shared = first_way(z_rt[...], y_rt[...], f_rt, row_rt, every)
    pending += shared
    up_tok.wait_recv()
    moved_low, shared = first_way(z_tok[:, :, low], y_tok[...], f0_tok, row_tok, low)
    pending += shared
    by_tok.wait_recv()
    moved_high, shared = second_way(z_tok[:, :, high], x_tok[...], f1_tok, row_tok, high)
    pending += shared
    arrived(deep_cot)
    up_cot = net.push(z_cot.at[:, :, low], y_cot, net.across)
    by_cot = net.push(z_cot.at[:, :, high], x_cot, net.beside)
    moved_rt.wait_recv()
    pending += share(row_rt.at[core, 1 - x])
    moved_low.wait_recv()
    pending += share(row_tok.at[core, 1 - x, :, :, low])
    moved_high.wait_recv()
    pending += share(row_tok.at[core, :, 1 - y, :, high])
    up_cot.wait_recv()
    moved_low, shared = first_way(z_cot[:, :, low], y_cot[...], f0_cot, row_cot, low)
    pending += shared
    by_cot.wait_recv()
    moved_high, shared = second_way(z_cot[:, :, high], x_cot[...], f1_cot, row_cot, high)
    pending += shared
    moved_low.wait_recv()
    pending += share(row_cot.at[core, 1 - x, :, :, low])
    moved_high.wait_recv()
    pending += share(row_cot.at[core, :, 1 - y, :, high])
    arrived(pending)
    net.finish()


def dispatch(experts, group, top, capacity, routing, tokens, cotangent):
    depth = experts // 4
    count, width = tokens.shape
    span, half = depth * capacity, width // 2
    bf16 = jnp.bfloat16
    order = jnp.arange(depth * count, dtype=jnp.int32)
    block = order // count
    tri = ((order[None, :] < order[:, None]) & (block[None, :] == block[:, None])).astype(bf16)
    kcap = jnp.broadcast_to((block * capacity).astype(jnp.float32)[:, None], (depth * count, LANES))
    vmem = pl.BlockSpec(memory_space=pltpu.VMEM)
    dense = [pltpu.VMEM((depth, count, w), bf16) for w in (LANES, width, width) + (LANES, half, half) * 2]
    routed = [pltpu.VMEM((2, span, w), bf16) for w in (LANES, half, half, half, half)]
    copies = 3 * (depth - 1) + 6 + 5 + 10 * (group - 1)
    return pl.pallas_call(
        functools.partial(dispatch_kernel, depth, group, top),
        out_shape=[
            jax.ShapeDtypeStruct((group, 2, 2, span, LANES), bf16),
            jax.ShapeDtypeStruct((group, 2, 2, span, width), bf16),
            jax.ShapeDtypeStruct((group, 2, 2, span, width), bf16),
            jax.ShapeDtypeStruct((4, 2, depth * count, LANES), bf16),
        ],
        in_specs=[vmem] * 5,
        out_specs=[vmem] * 4,
        scratch_shapes=dense + routed + [
            pltpu.SemaphoreType.DMA((3,)),
            pltpu.SemaphoreType.DMA((copies,)),
            pltpu.SemaphoreType.DMA((copies,)),
        ],
        compiler_params=pltpu.CompilerParams(
            collective_id=0, has_side_effects=True, vmem_limit_bytes=VMEM_LIMIT
        ),
    )(routing, tokens, cotangent, tri, kcap)


JOBS = ((0, 0), (1, 0), (1, 1), (2, 0), (2, 1))


def combine_kernel(depth, group, *refs):
    tabs, parts, outs = refs[0], refs[1:4], refs[4:7]
    bufs = refs[7 : 7 + 8 * len(JOBS)]
    send_sem, recv_sem = refs[7 + 8 * len(JOBS) :]
    net = Net(depth, group, send_sem, recv_sem)
    z, y, x, core = net.z, net.y, net.x, net.core
    net.barrier()

    class Job:
        pass

    jobs = []
    for number, (source, kind) in enumerate(JOBS):
        job = Job()
        job.part, job.out, job.kind = parts[source], outs[source], kind
        (job.mate, job.give, job.own, job.take, job.far, job.near, job.came, job.deep) = bufs[8 * number : 8 * number + 8]
        width = job.give.shape[-1]
        job.cols = pl.ds(kind * width, width)
        job.first, job.second = (net.beside, net.across) if kind == 0 else (net.across, net.beside)
        job.tabs = 2 * kind
        jobs.append(job)

    def pick(ref, lead, job, remote, cols):
        if job.kind == 0:
            return ref.at[lead, 1 - x if remote else x, :, :, cols]
        return ref.at[lead, :, 1 - y if remote else y, :, cols]

    every = lambda job: pl.ds(0, job.give.shape[-1])

    def exchange(job, remote):
        return [
            net.push(pick(job.part, (core + k) % group, job, remote, job.cols), pick(job.mate, k - 1, job, remote, every(job)), net.mates[k - 1])
            for k in range(1, group)
        ]

    def total(job, remote):
        acc = pick(job.part, core, job, remote, job.cols)[...].astype(jnp.float32)
        for k in range(1, group):
            acc = acc + pick(job.mate, k - 1, job, remote, every(job))[...].astype(jnp.float32)
        return acc.astype(jnp.bfloat16)

    def spread(job, part):
        rows = 2 * job.give.shape[1]
        mine = dot_f32(tabs[job.tabs, part, :, :rows], flat(job.own[...]))
        theirs = dot_f32(tabs[job.tabs + 1, part, :, :rows], flat(job.take[...]))
        return (mine + theirs).reshape(job.far.shape)

    for job in jobs:
        job.m1 = exchange(job, True)
    for job in jobs:
        job.m0 = exchange(job, False)
    for job in jobs:
        arrived(job.m1)
        job.give[...] = total(job, True)
        job.c1 = net.push(job.give, job.take, job.first)
    for job in jobs:
        arrived(job.m0)
        job.own[...] = total(job, False)
    for job in jobs:
        job.c1.wait_recv()
        job.far[...] = spread(job, 1).astype(jnp.bfloat16)
        job.c2 = net.push(job.far, job.came, job.second)
        job.near[...] = spread(job, 0).astype(jnp.bfloat16)
    for job in jobs:
        job.c2.wait_recv()
        job.near[...] = (job.near[...].astype(jnp.float32) + job.came[...].astype(jnp.float32)).astype(jnp.bfloat16)
        job.c3 = [
            net.push(job.near.at[(z + k) % depth], job.deep.at[z], net.deep[k - 1]) for k in range(1, depth)
        ]
    for job in jobs:
        arrived(job.c3)
        acc = job.near[z].astype(jnp.float32)
        for k in range(1, depth):
            acc = acc + job.deep[(z + k) % depth].astype(jnp.float32)
        job.out[:, job.cols] = acc.astype(job.out.dtype)
    net.finish()


def combine(experts, group, capacity, count, tabs, parts):
    depth = experts // 4
    width = parts[1].shape[-1]
    span, half = depth * capacity, width // 2
    bf16 = jnp.bfloat16
    vmem = pl.BlockSpec(memory_space=pltpu.VMEM)
    bufs = []
    for source, kind in JOBS:
        w = LANES if source == 0 else half
        bufs += [pltpu.VMEM((max(1, group - 1), 2, 2, span, w), bf16)]
        bufs += [pltpu.VMEM((2, span, w), bf16)] * 3
        bufs += [pltpu.VMEM((depth, count, w), bf16)] * 4
    copies = len(JOBS) * (2 * (group - 1) + 2 + depth - 1)
    return pl.pallas_call(
        functools.partial(combine_kernel, depth, group),
        out_shape=[
            jax.ShapeDtypeStruct((count, LANES), jnp.float32),
            jax.ShapeDtypeStruct((count, width), bf16),
            jax.ShapeDtypeStruct((count, width), bf16),
        ],
        in_specs=[vmem] * 4,
        out_specs=[vmem] * 3,
        scratch_shapes=bufs + [
            pltpu.SemaphoreType.DMA((copies,)),
            pltpu.SemaphoreType.DMA((copies,)),
        ],
        compiler_params=pltpu.CompilerParams(
            collective_id=1, has_side_effects=True, vmem_limit_bytes=VMEM_LIMIT
        ),
    )(tabs, *parts)


def per_device(tokens, cotangent, route_gates, routes, w_gate, w_up, w_down):
    experts, group = lax.axis_size("expert"), lax.axis_size("dp")
    token_count, top_count = routes.shape
    width = tokens.shape[1]
    capacity = max(2, token_count * top_count * 4 // (3 * experts))
    slots = experts * group * capacity
    gate_shard, up_shard, down_shard = (w_gate[0], w_up[0], w_down[0])
    me = lax.axis_index("expert")

    routing = jnp.concatenate([routes.astype(jnp.bfloat16), route_gates], axis=1)
    routing = jnp.pad(routing, ((0, 0), (0, LANES - 2 * top_count)))
    row_rt, row_tok, row_cot, tabs = dispatch(experts, group, top_count, capacity, routing, tokens, cotangent)
    shape = row_tok.shape
    row_rt = row_rt.reshape(slots, LANES).astype(jnp.float32)
    rows_in, rows_cot = row_tok.reshape(slots, width), row_cot.reshape(slots, width)
    named = row_rt[:, :top_count] == me.astype(jnp.float32)
    row_gate = jnp.sum(jnp.where(named, row_rt[:, top_count : 2 * top_count], 0.0), axis=1)[:, None]

    gate_pre = dot_f32(rows_in, gate_shard, INNER)
    up_pre = dot_f32(rows_in, up_shard, INNER)
    sig = jax.nn.sigmoid(gate_pre)
    hidden = (gate_pre * sig * up_pre).astype(jnp.bfloat16)
    out_rows = dot_f32(hidden, down_shard)
    row_grad = jnp.sum(out_rows * rows_cot.astype(jnp.float32), axis=1)[:, None]
    out_part = (out_rows * row_gate).astype(jnp.bfloat16)
    lane = jnp.arange(LANES, dtype=jnp.int32)[None, :]
    row_high = row_grad.astype(jnp.bfloat16)
    row_low = (row_grad - row_high.astype(jnp.float32)).astype(jnp.bfloat16)
    zero = jnp.zeros((), jnp.bfloat16)
    grad_cols = jnp.where(lane == me, row_high, jnp.where(lane == LANES // 2 + me, row_low, zero))
    rows_back = (rows_cot.astype(jnp.float32) * row_gate).astype(jnp.bfloat16)
    back_hidden = dot_f32(rows_back, down_shard, INNER)
    grad_pre = (back_hidden * up_pre * sig * (1.0 + gate_pre * (1.0 - sig))).astype(jnp.bfloat16)
    grad_upv = (back_hidden * gate_pre * sig).astype(jnp.bfloat16)
    back_part = (dot_f32(grad_pre, gate_shard) + dot_f32(grad_upv, up_shard)).astype(jnp.bfloat16)
    gate_cols, mixed, token_grad = combine(
        experts, group, capacity, token_count, tabs,
        [grad_cols.reshape(shape[:4] + (LANES,)), out_part.reshape(shape), back_part.reshape(shape)],
    )
    grad_down = dot_f32(hidden, rows_back, OUTER)
    grad_gate = dot_f32(grad_pre, rows_in, OUTER)
    grad_up = dot_f32(grad_upv, rows_in, OUTER)
    column = lane[:, None, :] % (LANES // 2)
    gate_grad = jnp.sum(jnp.where(routes[:, :, None] == column, gate_cols[:, None, :], 0.0), axis=2)
    return (mixed, token_grad, gate_grad, grad_gate[None], grad_up[None], grad_down[None])


def solution(mesh):
    row = P(("expert", "dp"), None)
    wide = P("expert", "dp", None)
    return jax.shard_map(
        per_device,
        mesh=mesh,
        in_specs=(row, row, row, row, wide, wide, wide),
        out_specs=(row, row, row, wide, wide, wide),
        check_vma=False,
    )
```

profile of v0, /device:TPU:0, one launch (start us, length us, event | category | flops | bytes accessed | tf_op | source)
XLA Modules:
  0.0 125.1 jit_solution(2390649358409881967)
XLA Ops:
  0.6 0.0 copy-start
  0.7 0.8 convert_element_type.84
  1.5 0.1 copy.18
  1.6 0.8 copy.19
  2.4 0.7 fusion.22.refs_0_
  3.1 0.7 fusion.19.refs_3_
  3.8 0.7 broadcast_in_dim.76.refs_4_
  4.5 38.1 %shard_map.118 = (bf16[2,2,2,48,128]{4,3,2,1,0:T(8,128)(2,1)}, bf16[2,2,2,48,2048]{4,3,2,1,0:T(8,128)(2,1)}, bf16[2,2,2,48,2048]{4,3,2,1,0:T(8,128)(2,1)}, bf16[4,2,96,128]{3,2,1,0:T(8,128)(2,1)}) custom-call(bf16[24,128]{1,0:T(8,128)(2,1)} %fusion.22.refs_0_, bf16[24,2048]{1,0:T(8,128)(2,1)} %refs_1_.1, bf16[24,2048]{1,0:T(8,128)(2,1)} %refs_2_.1, ...), custom_call_target="tpu_custom_call" | custom-call | tf_op jit(solution)/shard_map/pallas_call | solution.py:183
  42.6 0.9 convert.2
  43.5 0.2 fusion.17
  43.7 0.1 mul.65
  43.8 0.0 copy-start.1
  43.8 4.1 %fusion.9 = f32[384,704]{0,1:T(8,128)S(1)} fusion(bf16[384,2048]{1,0:T(8,128)(2,1)} %bitcast.54, bf16[1,704,2048]{2,1,0:T(8,128)(2,1)} %param.12), kind=kOutput, calls=%fused_computation.17 | convolution fusion | flops 1107296256 | bytes 5537792 | tf_op jit(solution)/shard_map/dot_general | solution.py:17
  47.9 0.0 copy-done.1
  47.9 0.3 fusion
  48.2 0.0 copy-done
  48.2 0.0 copy-start.3
  48.2 0.0 copy-start.5
  48.3 1.7 %fusion.3 = f32[384,704]{0,1:T(8,128)S(1)} fusion(bf16[384,2048]{1,0:T(8,128)(2,1)S(1)} %bitcast.58, bf16[1,704,2048]{2,1,0:T(8,128)(2,1)S(1)} %copy-done), kind=kOutput, calls=%fused_computation.11 | convolution fusion | flops 1107296256 | bytes 5537792 | tf_op jit(solution)/shard_map/dot_general | solution.py:17
  49.9 0.0 copy-done.3
  49.9 0.6 copy-done.5
  50.5 2.9 %multiply_convert_fusion.2 = (bf16[384,704]{0,1:T(8,128)(2,1)}, bf16[384,704]{0,1:T(8,128)(2,1)S(1)}, bf16[384,704]{0,1:T(8,128)(2,1)S(1)}) fusion(f32[384,704]{0,1:T(8,128)S(1)} %fusion.3, f32[384,704]{0,1:T(8,128)S(1)} %fusion.9, bf16[384,2048]{1,0:T(8,128)(2,1)S(1)} %bitcast.56, bf16[1,704,2048]{2,1,0:T(8,128)(2,1)S(1)} %copy-done.5), kind=kOutput, calls=%fused_computation.24 | convolution fusion | flops 1111621632 | bytes 8241152 | tf_op jit(solution)/shard_map/dot_general | solution.py:17
  53.4 0.0 copy-start.7
  53.4 3.5 %multiply_convert_fusion = (bf16[384,2048]{1,0:T(8,128)(2,1)}, f32[384]{0:T(512)S(1)}, bf16[384,2048]{1,0:T(8,128)(2,1)}) fusion(f32[384]{0:T(512)S(1)} %fusion.17, bf16[2,2,2,48,2048]{4,3,2,1,0:T(8,128)(2,1)S(1)} %copy-done.1, bf16[384,704]{0,1:T(8,128)(2,1)S(1)} %get-tuple-element.25, bf16[1,704,2048]{2,1,0:T(8,128)(2,1)S(1)} %copy-done), kind=kOutput, calls=%fused_computation.10 | convolution fusion | flops 1112800896 | bytes 8145920 | tf_op jit(solution)/shard_map/dot_general | solution.py:17
  56.9 0.0 copy-done.7
  56.9 0.1 reduce_sum.30
  57.0 0.8 select_select_fusion.refs_1_
  57.8 0.0 copy-start.6
  57.8 0.0 copy-start.9
  57.8 3.4 %fusion.7 = f32[384,2048]{1,0:T(8,128)S(1)} fusion(bf16[384,704]{0,1:T(8,128)(2,1)S(1)} %get-tuple-element.26, bf16[1,704,2048]{2,1,0:T(8,128)(2,1)} %param.12), kind=kOutput, calls=%fused_computation.15 | convolution fusion | flops 1107296256 | bytes 6569984 | tf_op jit(solution)/shard_map/dot_general | solution.py:17
  61.2 0.0 copy-done.6
  61.2 0.0 copy-done.9
  61.2 2.7 %add_convert_fusion = bf16[384,2048]{1,0:T(8,128)(2,1)} fusion(f32[384,2048]{1,0:T(8,128)S(1)} %fusion.7, bf16[384,704]{0,1:T(8,128)(2,1)S(1)} %copy-done.9, bf16[1,704,2048]{2,1,0:T(8,128)(2,1)S(1)} %copy-done.6), kind=kOutput, calls=%fused_computation.9 | convolution fusion | flops 1108869120 | bytes 8142848 | tf_op jit(solution)/shard_map/dot_general | solution.py:17
  63.9 0.0 copy-start.12
  63.9 44.3 %shard_map.119 = (f32[24,128]{1,0:T(8,128)}, bf16[24,2048]{1,0:T(8,128)(2,1)}, bf16[24,2048]{1,0:T(8,128)(2,1)}) custom-call(bf16[4,2,96,128]{3,2,1,0:T(8,128)(2,1)} %get-tuple-element.13.refs_0_, bf16[2,2,2,48,128]{4,3,2,1,0:T(8,128)(2,1)} %select_select_fusion.refs_1_, bf16[2,2,2,48,2048]{4,3,2,1,0:T(8,128)(2,1)} %bitcast.52, ...), custom_call_target="tpu_custom_call" | custom-call | tf_op jit(solution)/shard_map/pallas_call | solution.py:298
  108.2 0.0 copy-done.12
  108.2 1.5 %select_reduce_fusion = f32[24,6]{0,1:T(8,128)} fusion(f32[24,128]{1,0:T(8,128)} %get-tuple-element.19, s32[128]{0:T(128)S(1)} %and_select_fusion, s32[24,6]{0,1:T(8,128)S(1)} %copy-done.12), kind=kLoop, calls=%fused_computation.31 | loop fusion | flops 55152 | bytes 13952 | tf_op jit(solution)/shard_map/reduce_sum | solution.py:360
  109.7 0.0 copy-start.4
  109.7 5.7 %convolution_bitcast_fusion.2 = f32[1,704,2048]{2,1,0:T(8,128)} fusion(bf16[384,704]{0,1:T(8,128)(2,1)S(1)} %copy-done.9, bf16[384,2048]{1,0:T(8,128)(2,1)} %bitcast.55), kind=kOutput, calls=%fused_computation.2 | convolution fusion | flops 1107296256 | bytes 7880704 | tf_op jit(solution)/shard_map/dot_general | solution.py:17
  115.4 0.0 copy-done.4
  115.4 4.2 %convolution_bitcast_fusion.1 = f32[1,704,2048]{2,1,0:T(8,128)} fusion(bf16[384,704]{0,1:T(8,128)(2,1)S(1)} %get-tuple-element.26, bf16[384,2048]{1,0:T(8,128)(2,1)S(1)} %bitcast.57), kind=kOutput, calls=%fused_computation.1 | convolution fusion | flops 1107296256 | bytes 7880704 | tf_op jit(solution)/shard_map/dot_general | solution.py:17
  119.6 0.0 copy-done.2
  119.6 0.0 copy-done.8
  119.6 4.2 %convolution_bitcast_fusion = f32[1,704,2048]{2,1,0:T(8,128)} fusion(bf16[384,704]{0,1:T(8,128)(2,1)S(1)} %copy-done.8, bf16[384,2048]{1,0:T(8,128)(2,1)S(1)} %copy-done.2), kind=kOutput, calls=%fused_computation | convolution fusion | flops 1107296256 | bytes 7880704 | tf_op jit(solution)/shard_map/dot_general | solution.py:17
  123.8 0.0 copy-done.11
  123.8 0.6 copy.22
  124.5 0.0 copy-done.10
  124.5 0.6 copy.23
  (9 shorter events, 0.0 us)
Async XLA Ops:
  0.6 47.6 %copy-start = (bf16[1,704,2048]{2,1,0:T(8,128)(2,1)S(1)}, bf16[1,704,2048]{2,1,0:T(8,128)(2,1)}, u32[]{:S(2)}) copy-start(bf16[1,704,2048]{2,1,0:T(8,128)(2,1)} %param.13) | copy-start | bytes 8650756
  43.8 4.1 %copy-start.1 = (bf16[2,2,2,48,2048]{4,3,2,1,0:T(8,128)(2,1)S(1)}, bf16[2,2,2,48,2048]{4,3,2,1,0:T(8,128)(2,1)}, u32[]{:S(2)}) copy-start(bf16[2,2,2,48,2048]{4,3,2,1,0:T(8,128)(2,1)} %get-tuple-element.15) | copy-start | bytes 4718596
  48.2 1.7 %copy-start.3 = (bf16[2,2,2,48,2048]{4,3,2,1,0:T(8,128)(2,1)S(1)}, bf16[2,2,2,48,2048]{4,3,2,1,0:T(8,128)(2,1)}, u32[]{:S(2)}) copy-start(bf16[2,2,2,48,2048]{4,3,2,1,0:T(8,128)(2,1)} %get-tuple-element.14) | copy-start | bytes 4718596
  48.2 2.3 %copy-start.5 = (bf16[1,704,2048]{2,1,0:T(8,128)(2,1)S(1)}, bf16[1,704,2048]{2,1,0:T(8,128)(2,1)}, u32[]{:S(2)}) copy-start(bf16[1,704,2048]{2,1,0:T(8,128)(2,1)} %param.11) | copy-start | bytes 8650756
  53.4 3.5 %copy-start.7 = (bf16[384,704]{0,1:T(8,128)(2,1)}, bf16[384,704]{0,1:T(8,128)(2,1)S(1)}, u32[]{:S(2)}) copy-start(bf16[384,704]{0,1:T(8,128)(2,1)S(1)} %get-tuple-element.25) | copy-start | bytes 1622020
  57.8 3.4 %copy-start.6 = (bf16[1,704,2048]{2,1,0:T(8,128)(2,1)S(1)}, bf16[1,704,2048]{2,1,0:T(8,128)(2,1)}, u32[]{:S(2)}) copy-start(bf16[1,704,2048]{2,1,0:T(8,128)(2,1)} %param.11) | copy-start | bytes 8650756
  57.8 3.4 %copy-start.9 = (bf16[384,704]{0,1:T(8,128)(2,1)S(1)}, bf16[384,704]{0,1:T(8,128)(2,1)}, u32[]{:S(2)}) copy-start(bf16[384,704]{0,1:T(8,128)(2,1)} %get-tuple-element.24) | copy-start | bytes 1622020
  63.9 44.3 %copy-start.12 = (s32[24,6]{0,1:T(8,128)S(1)}, s32[24,6]{0,1:T(8,128)}, u32[]{:S(2)}) copy-start(s32[24,6]{0,1:T(8,128)} %param.10) | copy-start | bytes 1732
  109.7 5.7 %copy-start.4 = (bf16[2,2,2,48,2048]{4,3,2,1,0:T(8,128)(2,1)S(1)}, bf16[2,2,2,48,2048]{4,3,2,1,0:T(8,128)(2,1)}, u32[]{:S(2)}) copy-start(bf16[2,2,2,48,2048]{4,3,2,1,0:T(8,128)(2,1)} %get-tuple-element.14) | copy-start | bytes 4718596
  115.4 4.2 %copy-start.2 = (bf16[384,2048]{1,0:T(8,128)(2,1)S(1)}, bf16[384,2048]{1,0:T(8,128)(2,1)}, u32[]{:S(2)}) copy-start(bf16[384,2048]{1,0:T(8,128)(2,1)} %get-tuple-element.27) | copy-start | bytes 4718596
  115.4 4.2 %copy-start.8 = (bf16[384,704]{0,1:T(8,128)(2,1)S(1)}, bf16[384,704]{0,1:T(8,128)(2,1)}, u32[]{:S(2)}) copy-start(bf16[384,704]{0,1:T(8,128)(2,1)} %copy-done.7) | copy-start | bytes 1622020
  119.6 4.2 %copy-start.11 = (bf16[24,2048]{1,0:T(8,128)(2,1)S(1)}, bf16[24,2048]{1,0:T(8,128)(2,1)}, u32[]{:S(2)}) copy-start(bf16[24,2048]{1,0:T(8,128)(2,1)} %get-tuple-element.36) | copy-start | bytes 294916
  119.6 4.8 %copy-start.10 = (bf16[24,2048]{1,0:T(8,128)(2,1)S(1)}, bf16[24,2048]{1,0:T(8,128)(2,1)}, u32[]{:S(2)}) copy-start(bf16[24,2048]{1,0:T(8,128)(2,1)} %get-tuple-element.37) | copy-start | bytes 294916
where the time goes:
time: 125 us
  Pallas kernels  82.4 us (66%)
  matrix products  32.3 us (26%)
  other arithmetic  5.98 us (5%)
  local copies, waits for them, and re-layouts  3.66 us (3%)
    pallas_call x1, Pallas kernels, combine(): pl.pallas_call(functools.partial(combine_kernel, depth, group), out_shape...  44.3 us
    pallas_call x1, Pallas kernels, dispatch(): pl.pallas_call(functools.partial(dispatch_kernel, depth, group, top), out...  38.1 us
    dot_general x9, matrix products, dot_f32(): lax.dot_general(left, right, dims, preferred_element_type=jnp.float32)  32.3 us
    unnamed x29, local copies, waits for them, and re-layouts  2.69 us

commit v1 on v0

v1 whole, which is shorter than its diff:
```python
import functools

import jax
import jax.numpy as jnp
from jax import lax
from jax.experimental import pallas as pl
from jax.experimental.pallas import tpu as pltpu
from jax.sharding import PartitionSpec as P

INNER = (((1,), (1,)), ((), ()))
OUTER = (((0,), (0,)), ((), ()))
LANES = 128
VMEM_LIMIT = 60 * 1024 * 1024
FUSED_LIMIT = 4 * 1024 * 1024


def dot_f32(left, right, dims=(((1,), (0,)), ((), ()))):
    return lax.dot_general(left, right, dims, preferred_element_type=jnp.float32)


class Net:
    def __init__(self, depth, group, send_sem, recv_sem):
        me, core = lax.axis_index("expert"), lax.axis_index("dp")
        z, y, x = me // 4, (me // 2) % 2, me % 2
        self.me, self.core, self.z, self.y, self.x = me, core, z, y, x

        def at(zz, yy, xx, cc):
            return (zz * 4 + yy * 2 + xx, cc)

        self.deep = [at((z + k) % depth, y, x, core) for k in range(1, depth)]
        self.across, self.beside = at(z, 1 - y, x, core), at(z, y, 1 - x, core)
        self.mates = [at(z, y, x, (core + k) % group) for k in range(1, group)]
        self.across_id, self.beside_id = self.across[0], self.beside[0]
        self.send_sem, self.recv_sem = send_sem, recv_sem
        self.sent, self.used = [], 0

    def barrier(self):
        peers = self.deep + [self.across, self.beside] + self.mates
        barrier = pltpu.get_barrier_semaphore()
        for peer in peers:
            pl.semaphore_signal(barrier, inc=1, device_id=peer, device_id_type=pl.DeviceIdType.MESH)
        pl.semaphore_wait(barrier, len(peers))

    def push(self, src, dst, peer):
        index = self.used
        self.used += 1
        copy = pltpu.make_async_remote_copy(
            src_ref=src, dst_ref=dst, send_sem=self.send_sem.at[index], recv_sem=self.recv_sem.at[index],
            device_id=peer, device_id_type=pl.DeviceIdType.MESH,
        )
        copy.start()
        self.sent.append(copy)
        return copy

    def finish(self):
        for copy in self.sent:
            copy.wait_send()


def arrived(copies):
    for copy in copies:
        copy.wait_recv()


def flat(value):
    return value.reshape(-1, value.shape[-1])


class Dispatch:
    def __init__(self, net, top, ins, rows, tabs, dense, routed, own_sem):
        self.net, self.top, self.ins, self.rows, self.tabs = net, top, ins, rows, tabs
        self.near, self.up, self.by = dense[:3], dense[3:6], dense[6:9]
        self.send0, self.send1 = (routed[0], routed[1], routed[2]), (None, routed[3], routed[4])
        self.own_sem = own_sem
        half = ins[1].shape[1] // 2
        self.low = (pl.ds(0, LANES), pl.ds(0, half), pl.ds(0, half))
        self.high = pl.ds(half, half)
        self.span = rows[0].shape[3]
        self.pending = []
        self.moved0, self.moved1, self.deep, self.side0, self.side1 = {}, {}, {}, {}, {}

    def start(self):
        net = self.net
        own = []
        for t in range(3):
            copy = pltpu.make_async_copy(self.ins[t], self.near[t].at[net.z], self.own_sem.at[t])
            copy.start()
            own.append(copy)
        self.push_deep(0)
        self.push_deep(1)
        for copy in own:
            copy.wait()

    def push_deep(self, t):
        net = self.net
        self.deep[t] = [net.push(self.ins[t], self.near[t].at[net.z], peer) for peer in net.deep]

    def push_side(self, t):
        net = self.net
        arrived(self.deep[t])
        if t == 0:
            self.side0[t] = net.push(self.near[t], self.up[t], net.across)
            self.side1[t] = net.push(self.near[t], self.by[t], net.beside)
        else:
            self.side0[t] = net.push(self.near[t].at[:, :, self.low[t]], self.up[t], net.across)
            self.side1[t] = net.push(self.near[t].at[:, :, self.high], self.by[t], net.beside)

    def tables(self):
        net, span, count = self.net, self.span, self.ins[0].shape[0]
        self.side0[0].wait_recv()
        self.side1[0].wait_recv()
        depth = self.near[0].shape[0]
        total = depth * count
        lane = lax.broadcasted_iota(jnp.int32, (total, LANES), 1)
        row = lax.broadcasted_iota(jnp.int32, (total, LANES), 0)
        down, right = lax.broadcasted_iota(jnp.int32, (total, total), 0), lax.broadcasted_iota(jnp.int32, (total, total), 1)
        kcap = jnp.zeros((total, LANES), jnp.int32)
        first = jnp.zeros((total, total), jnp.int32)
        for k in range(1, depth):
            kcap = jnp.where(row >= k * count, k * (span // depth), kcap)
            first = jnp.where(down >= k * count, k * count, first)
        tri = ((right < down) & (right >= first)).astype(jnp.float32).astype(jnp.bfloat16)

        def table(which, part, source, expert, base):
            routing = flat(source[...]).astype(jnp.float32)
            named = (routing == expert.astype(jnp.float32)) & (lane < self.top)
            used = jnp.sum(named.astype(jnp.float32), axis=1, keepdims=True)
            used = jnp.broadcast_to(used, lane.shape)
            rank = dot_f32(tri, used.astype(jnp.bfloat16))
            slot = rank + (kcap + base * span).astype(jnp.float32)
            hit = (used > 0.5) & (slot == lane.astype(jnp.float32))
            self.tabs[which, part] = hit.astype(jnp.float32).astype(jnp.bfloat16)

        z_rt, y_rt, x_rt = self.near[0], self.up[0], self.by[0]
        table(0, 0, z_rt, net.me, net.y)
        table(0, 1, y_rt, net.me, 1 - net.y)
        table(1, 0, z_rt, net.beside_id, net.y)
        table(1, 1, y_rt, net.beside_id, 1 - net.y)
        table(2, 0, z_rt, net.me, net.x)
        table(2, 1, x_rt, net.me, 1 - net.x)
        table(3, 0, z_rt, net.across_id, net.x)
        table(3, 1, x_rt, net.across_id, 1 - net.x)

    def chosen(self, which, near, far):
        rows = dot_f32(self.tabs[which, 0], flat(near), OUTER) + dot_f32(self.tabs[which, 1], flat(far), OUTER)
        return rows[: 2 * self.span].astype(jnp.bfloat16).reshape(2, self.span, -1)

    def share(self, view):
        self.pending += [self.net.push(view, view, peer) for peer in self.net.mates]

    def first_way(self, t):
        net, cols, send, rows = self.net, self.low[t], self.send0[t], self.rows[t]
        self.side0[t].wait_recv() if t else None
        near, far = self.near[t][:, :, cols], self.up[t][...]
        send[...] = self.chosen(1, near, far)
        self.moved0[t] = net.push(send, rows.at[net.core, net.x, :, :, cols], net.beside)
        rows[net.core, net.x, :, :, cols] = self.chosen(0, near, far)
        self.share(rows.at[net.core, net.x, :, :, cols])

    def second_way(self, t):
        net, cols, send, rows = self.net, self.high, self.send1[t], self.rows[t]
        self.side1[t].wait_recv()
        near, far = self.near[t][:, :, cols], self.by[t][...]
        send[...] = self.chosen(3, near, far)
        self.moved1[t] = net.push(send, rows.at[net.core, :, net.y, :, cols], net.across)
        rows[net.core, :, net.y, :, cols] = self.chosen(2, near, far)
        self.share(rows.at[net.core, :, net.y, :, cols])

    def last(self, t):
        net, rows = self.net, self.rows[t]
        self.moved0[t].wait_recv()
        self.share(rows.at[net.core, 1 - net.x, :, :, self.low[t]])
        if t:
            self.moved1[t].wait_recv()
            self.share(rows.at[net.core, :, 1 - net.y, :, self.high])

    def settle(self):
        arrived(self.pending)
        self.pending = []


def dispatch_kernel(depth, group, top, *refs):
    ins, rows, tabs = refs[:3], refs[3:6], refs[6]
    own_sem, send_sem, recv_sem = refs[21:]
    net = Net(depth, group, send_sem, recv_sem)
    step = Dispatch(net, top, ins, rows, tabs, refs[7:16], refs[16:21], own_sem)
    net.barrier()
    step.start()
    step.push_side(0)
    step.push_side(1)
    step.push_deep(2)
    step.tables()
    step.first_way(0)
    step.first_way(1)
    step.second_way(1)
    step.push_side(2)
    step.last(0)
    step.last(1)
    step.first_way(2)
    step.second_way(2)
    step.last(2)
    step.settle()
    net.finish()


def dispatch_scratch(depth, count, span, width):
    half, bf16 = width // 2, jnp.bfloat16
    dense = [pltpu.VMEM((depth, count, w), bf16) for w in (LANES, width, width) + (LANES, half, half) * 2]
    return dense + [pltpu.VMEM((2, span, w), bf16) for w in (LANES, half, half, half, half)]


def dispatch_copies(depth, group):
    return 3 * (depth - 1) + 6 + 5 + 10 * (group - 1)


def semaphores(copies):
    return [pltpu.SemaphoreType.DMA((copies,)), pltpu.SemaphoreType.DMA((copies,))]


VMEM_SPEC = pl.BlockSpec(memory_space=pltpu.VMEM)
ANY_SPEC = pl.BlockSpec(memory_space=pl.ANY)


def dispatch(experts, group, top, capacity, routing, tokens, cotangent):
    depth = experts // 4
    count, width = tokens.shape
    span = depth * capacity
    bf16 = jnp.bfloat16
    return pl.pallas_call(
        functools.partial(dispatch_kernel, depth, group, top),
        out_shape=[
            jax.ShapeDtypeStruct((group, 2, 2, span, LANES), bf16),
            jax.ShapeDtypeStruct((group, 2, 2, span, width), bf16),
            jax.ShapeDtypeStruct((group, 2, 2, span, width), bf16),
            jax.ShapeDtypeStruct((4, 2, depth * count, LANES), bf16),
        ],
        in_specs=[VMEM_SPEC] * 3,
        out_specs=[VMEM_SPEC] * 4,
        scratch_shapes=dispatch_scratch(depth, count, span, width)
        + [pltpu.SemaphoreType.DMA((3,))]
        + semaphores(dispatch_copies(depth, group)),
        compiler_params=pltpu.CompilerParams(
            collective_id=0, has_side_effects=True, vmem_limit_bytes=VMEM_LIMIT
        ),
    )(routing, tokens, cotangent)


JOBS = ((0, 0), (1, 0), (1, 1), (2, 0), (2, 1))


class Job:
    def __init__(self, net, depth, group, tabs, part, out, kind, bufs):
        self.net, self.depth, self.group, self.tabs = net, depth, group, tabs
        self.part, self.out, self.kind = part, out, kind
        (self.mate, self.give, self.own, self.take, self.far, self.near, self.came, self.deep) = bufs
        width = self.give.shape[-1]
        self.cols, self.every = pl.ds(kind * width, width), pl.ds(0, width)
        self.first, self.second = (net.beside, net.across) if kind == 0 else (net.across, net.beside)

    def pick(self, ref, lead, remote, cols):
        net = self.net
        if self.kind == 0:
            return ref.at[lead, 1 - net.x if remote else net.x, :, :, cols]
        return ref.at[lead, :, 1 - net.y if remote else net.y, :, cols]

    def exchange(self):
        net, group = self.net, self.group
        self.copies0 = []
        for remote in (True, False):
            self.copies0.append([
                net.push(
                    self.pick(self.part, (net.core + k) % group, remote, self.cols),
                    self.pick(self.mate, k - 1, remote, self.every),
                    net.mates[k - 1],
                )
                for k in range(1, group)
            ])

    def total(self, remote):
        acc = self.pick(self.part, self.net.core, remote, self.cols)[...].astype(jnp.float32)
        for k in range(1, self.group):
            acc = acc + self.pick(self.mate, k - 1, remote, self.every)[...].astype(jnp.float32)
        return acc.astype(jnp.bfloat16)

    def hop1(self):
        arrived(self.copies0[0])
        self.give[...] = self.total(True)
        self.copy1 = self.net.push(self.give, self.take, self.first)

    def keep(self):
        arrived(self.copies0[1])
        self.own[...] = self.total(False)

    def spread(self, part):
        rows, which = 2 * self.give.shape[1], 2 * self.kind
        mine = dot_f32(self.tabs[which, part, :, :rows], flat(self.own[...]))
        theirs = dot_f32(self.tabs[which + 1, part, :, :rows], flat(self.take[...]))
        return (mine + theirs).astype(jnp.bfloat16).reshape(self.far.shape)

    def hop2(self):
        self.copy1.wait_recv()
        self.far[...] = self.spread(1)
        self.copy2 = self.net.push(self.far, self.came, self.second)
        self.near[...] = self.spread(0)

    def hop3(self):
        net, depth = self.net, self.depth
        self.copy2.wait_recv()
        self.near[...] = (self.near[...].astype(jnp.float32) + self.came[...].astype(jnp.float32)).astype(jnp.bfloat16)
        self.copies3 = [
            net.push(self.near.at[(net.z + k) % depth], self.deep.at[net.z], net.deep[k - 1]) for k in range(1, depth)
        ]

    def sum(self):
        z, depth = self.net.z, self.depth
        arrived(self.copies3)
        acc = self.near[z].astype(jnp.float32)
        for k in range(1, depth):
            acc = acc + self.deep[(z + k) % depth].astype(jnp.float32)
        return acc

    def home(self):
        self.out[:, self.cols] = self.sum().astype(self.out.dtype)


def jobs_scratch(depth, group, count, span, width):
    bf16, half, bufs = jnp.bfloat16, width // 2, []
    for source, kind in JOBS:
        w = LANES if source == 0 else half
        bufs += [pltpu.VMEM((max(1, group - 1), 2, 2, span, w), bf16)]
        bufs += [pltpu.VMEM((2, span, w), bf16)] * 3
        bufs += [pltpu.VMEM((depth, count, w), bf16)] * 4
    return bufs


def jobs_copies(depth, group):
    return len(JOBS) * (2 * (group - 1) + 2 + depth - 1)


def make_jobs(net, depth, group, tabs, parts, outs, bufs):
    return [
        Job(net, depth, group, tabs, parts[source], outs[source], kind, bufs[8 * i : 8 * i + 8])
        for i, (source, kind) in enumerate(JOBS)
    ]


def combine_kernel(depth, group, *refs):
    tabs, parts, outs = refs[0], refs[1:4], refs[4:7]
    net = Net(depth, group, refs[-2], refs[-1])
    net.barrier()
    jobs = make_jobs(net, depth, group, tabs, parts, outs, refs[7:-2])
    for name in ("exchange", "hop1", "keep", "hop2", "hop3", "home"):
        for job in jobs:
            getattr(job, name)()
    net.finish()


def combine(experts, group, capacity, count, tabs, parts):
    depth = experts // 4
    width = parts[1].shape[-1]
    bf16 = jnp.bfloat16
    return pl.pallas_call(
        functools.partial(combine_kernel, depth, group),
        out_shape=[
            jax.ShapeDtypeStruct((count, LANES), jnp.float32),
            jax.ShapeDtypeStruct((count, width), bf16),
            jax.ShapeDtypeStruct((count, width), bf16),
        ],
        in_specs=[VMEM_SPEC] * 4,
        out_specs=[VMEM_SPEC] * 3,
        scratch_shapes=jobs_scratch(depth, group, count, depth * capacity, width)
        + semaphores(jobs_copies(depth, group)),
        compiler_params=pltpu.CompilerParams(
            collective_id=1, has_side_effects=True, vmem_limit_bytes=VMEM_LIMIT
        ),
    )(tabs, *parts)


def layer_kernel(depth, group, top, *refs):
    ins, (wg_hbm, wu_hbm, wd_hbm) = refs[:3], refs[3:6]
    (mixed, token_grad, gate_grad, row_tok, row_back, hid_t, pre_t, upv_t) = refs[6:14]
    (wg, wu, wd, row_rt, row_cot, tabs, row_gate, gp, up, bh, hid, pre, upv, ext_part, out_part, back_part, acc, gate_cols) = refs[14:32]
    dense, routed = refs[32:41], refs[41:46]
    weight_sem, own_sem, send_sem, recv_sem = refs[-4:]
    bufs = refs[46:-4]
    net = Net(depth, group, send_sem, recv_sem)
    step = Dispatch(net, top, ins, (row_rt, row_tok, row_cot), tabs, dense, routed, own_sem)
    jobs = make_jobs(net, depth, group, tabs, (ext_part, out_part, back_part), (gate_cols, mixed, token_grad), bufs)
    forward, back = jobs[:3], jobs[3:]
    slots, ff, width = gp.shape[0], wg.shape[0], wg.shape[1]
    lead = row_tok.shape[:4]
    chunk = 512
    net.barrier()
    weights = []
    for i, (src, dst) in enumerate(((wg_hbm, wg), (wu_hbm, wu), (wd_hbm, wd))):
        copy = pltpu.make_async_copy(src.at[0], dst, weight_sem.at[i])
        weights.append(copy)

    step.start()
    for copy in weights:
        copy.start()
    step.push_side(0)
    step.push_side(1)
    step.push_deep(2)
    step.tables()
    step.first_way(0)
    step.first_way(1)
    step.second_way(1)
    step.push_side(2)
    step.last(0)
    step.last(1)
    step.settle()

    lane = lax.broadcasted_iota(jnp.int32, (slots, LANES), 1)
    routing = row_rt[...].reshape(slots, LANES).astype(jnp.float32)
    gates = pltpu.roll(routing, LANES - top, 1)
    named = (routing == net.me.astype(jnp.float32)) & (lane < top)
    row_gate[...] = jnp.broadcast_to(jnp.sum(jnp.where(named, gates, 0.0), axis=1, keepdims=True), (slots, LANES))

    for copy in weights:
        copy.wait()
    gp[...] = dot_f32(row_tok[...].reshape(slots, width), wg[...], INNER)
    step.first_way(2)
    step.second_way(2)
    up[...] = dot_f32(row_tok[...].reshape(slots, width), wu[...], INNER)
    step.last(2)

    rows = 16

    @pl.loop(0, slots // rows)
    def _(i):
        at = pl.ds(pl.multiple_of(i * rows, rows), rows)
        g = gp[at, :]
        hid[at, pl.ds(0, ff)] = (g * jax.nn.sigmoid(g) * up[at, :]).astype(jnp.bfloat16)

    step.settle()
    acc[...] = jnp.zeros_like(acc)

    @pl.loop(0, width // chunk)
    def _(i):
        cols = pl.ds(pl.multiple_of(i * chunk, chunk), chunk)
        value = dot_f32(hid[:, :ff], wd[:, cols])
        cot = row_cot[:, :, :, :, cols].reshape(slots, chunk).astype(jnp.float32)
        product = value * cot
        for j in range(chunk // LANES):
            acc[...] += product[:, j * LANES : (j + 1) * LANES]
        gate = row_gate[:, :1]
        out_part[:, :, :, :, cols] = (value * gate).astype(jnp.bfloat16).reshape(lead + (chunk,))
        row_back[:, :, :, :, cols] = (cot * gate).astype(jnp.bfloat16).reshape(lead + (chunk,))

    row_grad = jnp.sum(acc[...], axis=1, keepdims=True)
    row_high = row_grad.astype(jnp.bfloat16).astype(jnp.float32)
    row_low = row_grad - row_high
    ext = jnp.where(lane == net.me, row_high, jnp.where(lane == LANES // 2 + net.me, row_low, 0.0))
    ext_part[...] = ext.astype(jnp.bfloat16).reshape(ext_part.shape)
    for job in forward:
        job.exchange()
    bh[...] = dot_f32(row_back[...].reshape(slots, width), wd[...], INNER)
    for name in ("hop1", "keep"):
        for job in forward:
            getattr(job, name)()

    @pl.loop(0, slots // rows)
    def _(i):
        at = pl.ds(pl.multiple_of(i * rows, rows), rows)
        g, b = gp[at, :], bh[at, :]
        s = jax.nn.sigmoid(g)
        pre[at, pl.ds(0, ff)] = (b * up[at, :] * s * (1.0 + g * (1.0 - s))).astype(jnp.bfloat16)
        upv[at, pl.ds(0, ff)] = (b * g * s).astype(jnp.bfloat16)

    def back_cols(first, last):
        @pl.loop(first, last)
        def _(i):
            cols = pl.ds(pl.multiple_of(i * chunk, chunk), chunk)
            value = dot_f32(pre[:, :ff], wg[:, cols]) + dot_f32(upv[:, :ff], wu[:, cols])
            back_part[:, :, :, :, cols] = value.astype(jnp.bfloat16).reshape(lead + (chunk,))

    for job in forward:
        job.hop2()
    middle = width // chunk // 2
    back_cols(0, middle)
    back[0].exchange()
    back_cols(middle, 2 * middle)
    back[1].exchange()
    for job in forward:
        job.hop3()
    for job in back:
        job.hop1()
    for job in back:
        job.keep()
    for src, dst in ((hid, hid_t), (pre, pre_t), (upv, upv_t)):
        dst[...] = src[...].T[:ff]
    for job in back:
        job.hop2()
    for job in back:
        job.hop3()
    for job in forward:
        job.home()
    count = gate_cols.shape[0]
    lane = lax.broadcasted_iota(jnp.int32, (count, LANES), 1)
    cols = gate_cols[...] + pltpu.roll(gate_cols[...], LANES // 2, 1)
    routing = dense[0][net.z].astype(jnp.float32)
    grads = jnp.zeros((count, LANES), jnp.float32)
    for k in range(top):
        hit = (routing[:, k : k + 1] == lane.astype(jnp.float32)) & (lane < LANES // 2)
        grads = jnp.where(lane == k, jnp.sum(jnp.where(hit, cols, 0.0), axis=1, keepdims=True), grads)
    gate_grad[...] = grads
    for job in back:
        job.home()
    net.finish()


def layer(experts, group, top, capacity, routing, tokens, cotangent, w_gate, w_up, w_down):
    depth = experts // 4
    count, width = tokens.shape
    ff = w_gate.shape[1]
    span = depth * capacity
    slots = group * 4 * span
    wide = -(-ff // LANES) * LANES
    bf16, f32 = jnp.bfloat16, jnp.float32
    blocks = (group, 2, 2, span)
    scratch = [
        pltpu.VMEM((ff, width), bf16), pltpu.VMEM((ff, width), bf16), pltpu.VMEM((ff, width), bf16),
        pltpu.VMEM(blocks + (LANES,), bf16), pltpu.VMEM(blocks + (width,), bf16),
        pltpu.VMEM((4, 2, depth * count, LANES), bf16), pltpu.VMEM((slots, LANES), f32),
        pltpu.VMEM((slots, ff), f32), pltpu.VMEM((slots, ff), f32), pltpu.VMEM((slots, ff), f32),
        pltpu.VMEM((slots, wide), bf16), pltpu.VMEM((slots, wide), bf16), pltpu.VMEM((slots, wide), bf16),
        pltpu.VMEM(blocks + (LANES,), bf16), pltpu.VMEM(blocks + (width,), bf16), pltpu.VMEM(blocks + (width,), bf16),
        pltpu.VMEM((slots, LANES), f32), pltpu.VMEM((count, LANES), f32),
    ]
    copies = dispatch_copies(depth, group) + jobs_copies(depth, group)
    return pl.pallas_call(
        functools.partial(layer_kernel, depth, group, top),
        out_shape=[
            jax.ShapeDtypeStruct((count, width), bf16),
            jax.ShapeDtypeStruct((count, width), bf16),
            jax.ShapeDtypeStruct((count, LANES), f32),
            jax.ShapeDtypeStruct(blocks + (width,), bf16),
            jax.ShapeDtypeStruct(blocks + (width,), bf16),
        ] + [jax.ShapeDtypeStruct((ff, slots), bf16)] * 3,
        in_specs=[ANY_SPEC] * 6,
        out_specs=[VMEM_SPEC] * 8,
        scratch_shapes=scratch
        + dispatch_scratch(depth, count, span, width)
        + jobs_scratch(depth, group, count, span, width)
        + [pltpu.SemaphoreType.DMA((3,)), pltpu.SemaphoreType.DMA((3,))]
        + semaphores(copies),
        compiler_params=pltpu.CompilerParams(
            collective_id=2, has_side_effects=True, vmem_limit_bytes=VMEM_LIMIT
        ),
    )(routing, tokens, cotangent, w_gate, w_up, w_down)


def per_device(tokens, cotangent, route_gates, routes, w_gate, w_up, w_down):
    experts, group = lax.axis_size("expert"), lax.axis_size("dp")
    token_count, top_count = routes.shape
    width = tokens.shape[1]
    capacity = max(2, token_count * top_count * 4 // (3 * experts))
    slots = experts * group * capacity
    gate_shard, up_shard, down_shard = (w_gate[0], w_up[0], w_down[0])
    me = lax.axis_index("expert")

    routing = jnp.concatenate([routes.astype(jnp.bfloat16), route_gates], axis=1)
    routing = jnp.pad(routing, ((0, 0), (0, LANES - 2 * top_count)))
    if 2 * slots * width * tokens.dtype.itemsize <= FUSED_LIMIT:
        mixed, token_grad, gate_grad, rows_in, rows_back, hid_t, pre_t, upv_t = layer(
            experts, group, top_count, capacity, routing, tokens, cotangent, w_gate, w_up, w_down
        )
        rows_in, rows_back = rows_in.reshape(slots, width), rows_back.reshape(slots, width)
        grad_down = dot_f32(hid_t, rows_back)
        grad_gate = dot_f32(pre_t, rows_in)
        grad_up = dot_f32(upv_t, rows_in)
        return (mixed, token_grad, gate_grad[:, :top_count], grad_gate[None], grad_up[None], grad_down[None])
    row_rt, row_tok, row_cot, tabs = dispatch(experts, group, top_count, capacity, routing, tokens, cotangent)
    shape = row_tok.shape
    row_rt = row_rt.reshape(slots, LANES).astype(jnp.float32)
    rows_in, rows_cot = row_tok.reshape(slots, width), row_cot.reshape(slots, width)
    named = row_rt[:, :top_count] == me.astype(jnp.float32)
    row_gate = jnp.sum(jnp.where(named, row_rt[:, top_count : 2 * top_count], 0.0), axis=1)[:, None]

    gate_pre = dot_f32(rows_in, gate_shard, INNER)
    up_pre = dot_f32(rows_in, up_shard, INNER)
    sig = jax.nn.sigmoid(gate_pre)
    hidden = (gate_pre * sig * up_pre).astype(jnp.bfloat16)
    out_rows = dot_f32(hidden, down_shard)
    row_grad = jnp.sum(out_rows * rows_cot.astype(jnp.float32), axis=1)[:, None]
    out_part = (out_rows * row_gate).astype(jnp.bfloat16)
    lane = jnp.arange(LANES, dtype=jnp.int32)[None, :]
    row_high = row_grad.astype(jnp.bfloat16)
    row_low = (row_grad - row_high.astype(jnp.float32)).astype(jnp.bfloat16)
    zero = jnp.zeros((), jnp.bfloat16)
    grad_cols = jnp.where(lane == me, row_high, jnp.where(lane == LANES // 2 + me, row_low, zero))
    rows_back = (rows_cot.astype(jnp.float32) * row_gate).astype(jnp.bfloat16)
    back_hidden = dot_f32(rows_back, down_shard, INNER)
    grad_pre = (back_hidden * up_pre * sig * (1.0 + gate_pre * (1.0 - sig))).astype(jnp.bfloat16)
    grad_upv = (back_hidden * gate_pre * sig).astype(jnp.bfloat16)
    back_part = (dot_f32(grad_pre, gate_shard) + dot_f32(grad_upv, up_shard)).astype(jnp.bfloat16)
    gate_cols, mixed, token_grad = combine(
        experts, group, capacity, token_count, tabs,
        [grad_cols.reshape(shape[:4] + (LANES,)), out_part.reshape(shape), back_part.reshape(shape)],
    )
    grad_down = dot_f32(hidden, rows_back, OUTER)
    grad_gate = dot_f32(grad_pre, rows_in, OUTER)
    grad_up = dot_f32(grad_upv, rows_in, OUTER)
    column = lane[:, None, :] % (LANES // 2)
    gate_grad = jnp.sum(jnp.where(routes[:, :, None] == column, gate_cols[:, None, :], 0.0), axis=2)
    return (mixed, token_grad, gate_grad, grad_gate[None], grad_up[None], grad_down[None])


def solution(mesh):
    row = P(("expert", "dp"), None)
    wide = P("expert", "dp", None)
    return jax.shard_map(
        per_device,
        mesh=mesh,
        in_specs=(row, row, row, row, wide, wide, wide),
        out_specs=(row, row, row, wide, wide, wide),
        check_vma=False,
    )
```

time: 125 us -> 100 us (0.80)
  matrix products: 32.3 us -> 14.3 us
  other arithmetic: 5.98 us -> 1.37 us
  Pallas kernels: 82.4 us -> 79.9 us
    dot_general x9 -> x3, matrix products: 32.3 us -> 14.3 us  [dot_f32(): lax.dot_general(left, right, dims, preferred_element_type=jnp.float32)]
    pallas_call x2 -> x1, Pallas kernels: 82.4 us -> 79.9 us  [layer(): pl.pallas_call(functools.partial(layer_kernel, depth, group, top), out_sh...]
    convert_element_type x5 -> x0, other arithmetic: 1.94 us -> none  [the longest x1 0.91 us: per_device(): row_rt = row_rt.reshape(slots, LANES).astype(jnp.float32)]
    reduce_sum x2 -> x0, other arithmetic: 1.7 us -> none  [the longest x1 1.47 us: per_device(): jnp.sum(jnp.where(routes[:, :, None] == column, gate_cols[:, None, :], 0....]
    unnamed x29 -> x16, local copies, waits for them, and re-layouts: 2.69 us -> 3.45 us
where the time goes in v1:
time: 100 us; the launch traced here: 99.8 us
  Pallas kernels  79.9 us (80%)
  matrix products  14.3 us (14%)
  local copies, waits for them, and re-layouts  3.55 us (4%)
  other arithmetic  1.37 us (1%)
    pallas_call x1, Pallas kernels, layer(): pl.pallas_call(functools.partial(layer_kernel, depth, group, top), out_sh...  79.9 us
    dot_general x3, matrix products, dot_f32(): lax.dot_general(left, right, dims, preferred_element_type=jnp.float32)  14.3 us
    unnamed x16, local copies, waits for them, and re-layouts  3.45 us

profile of v1, /device:TPU:0, one launch (start us, length us, event | category | flops | bytes accessed | tf_op | source)
XLA Modules:
  0.0 99.8 jit_solution(11539738961099938153)
XLA Ops:
  0.6 0.7 convert_element_type.5
  1.3 0.1 copy.16
  1.4 0.8 copy.17
  2.2 0.7 fusion.2.refs_0_
  2.9 79.9 %shard_map.118 = (bf16[24,2048]{1,0:T(8,128)(2,1)}, bf16[24,2048]{1,0:T(8,128)(2,1)}, f32[24,128]{1,0:T(8,128)}, bf16[2,2,2,48,2048]{4,3,2,1,0:T(8,128)(2,1)}, b...) custom-call(bf16[24,128]{1,0:T(8,128)(2,1)} %fusion.2.refs_0_, ...), custom_call_target="tpu_custom_call" | custom-call | tf_op jit(solution)/shard_map/pallas_call | solution.py:532
  82.8 1.4 %copy.18 = f32[24,6]{0,1:T(8,128)} copy(f32[24,6]{1,0:T(8,128)} %bitcast.18) | data formatting | bytes 1152
  84.2 0.0 copy-start
  84.2 0.0 copy-start.3
  84.2 5.9 %convolution_bitcast_fusion.2 = f32[1,704,2048]{2,1,0:T(8,128)} fusion(bf16[704,384]{1,0:T(8,128)(2,1)} %get-tuple-element.17, bf16[384,2048]{1,0:T(8,128)(2,1)} %bitcast.15), kind=kOutput, calls=%fused_computation.2 | convolution fusion | flops 1107296256 | bytes 7880704 | tf_op jit(solution)/shard_map/dot_general | solution.py:18
  90.1 0.0 copy-done
  90.1 0.0 copy-done.3
  90.1 0.0 copy-start.1
  90.1 0.0 copy-start.2
  90.1 4.2 %convolution_bitcast_fusion.1 = f32[1,704,2048]{2,1,0:T(8,128)} fusion(bf16[704,384]{1,0:T(8,128)(2,1)S(1)} %copy-done.3, bf16[384,2048]{1,0:T(8,128)(2,1)S(1)} %bitcast.16), kind=kOutput, calls=%fused_computation.1 | convolution fusion | flops 1107296256 | bytes 7880704 | tf_op jit(solution)/shard_map/dot_general | solution.py:18
  94.3 0.0 copy-done.1
  94.3 0.0 copy-done.2
  94.3 0.0 copy-start.5
  94.3 0.0 copy-start.4
  94.3 4.2 %convolution_bitcast_fusion = f32[1,704,2048]{2,1,0:T(8,128)} fusion(bf16[704,384]{1,0:T(8,128)(2,1)S(1)} %copy-done.2, bf16[384,2048]{1,0:T(8,128)(2,1)S(1)} %bitcast.17), kind=kOutput, calls=%fused_computation | convolution fusion | flops 1107296256 | bytes 7880704 | tf_op jit(solution)/shard_map/dot_general | solution.py:18
  98.5 0.0 copy-done.5
  98.5 0.6 copy.21
  99.2 0.0 copy-done.4
  99.2 0.6 copy.22
Async XLA Ops:
  84.2 5.9 %copy-start = (bf16[2,2,2,48,2048]{4,3,2,1,0:T(8,128)(2,1)S(1)}, bf16[2,2,2,48,2048]{4,3,2,1,0:T(8,128)(2,1)}, u32[]{:S(2)}) copy-start(bf16[2,2,2,48,2048]{4,3,2,1,0:T(8,128)(2,1)} %get-tuple-element.18) | copy-start | bytes 4718596
  84.2 5.9 %copy-start.3 = (bf16[704,384]{1,0:T(8,128)(2,1)S(1)}, bf16[704,384]{1,0:T(8,128)(2,1)}, u32[]{:S(2)}) copy-start(bf16[704,384]{1,0:T(8,128)(2,1)} %get-tuple-element.19) | copy-start | bytes 1622020
  90.1 4.2 %copy-start.1 = (bf16[2,2,2,48,2048]{4,3,2,1,0:T(8,128)(2,1)S(1)}, bf16[2,2,2,48,2048]{4,3,2,1,0:T(8,128)(2,1)}, u32[]{:S(2)}) copy-start(bf16[2,2,2,48,2048]{4,3,2,1,0:T(8,128)(2,1)} %get-tuple-element.21) | copy-start | bytes 4718596
  90.1 4.2 %copy-start.2 = (bf16[704,384]{1,0:T(8,128)(2,1)S(1)}, bf16[704,384]{1,0:T(8,128)(2,1)}, u32[]{:S(2)}) copy-start(bf16[704,384]{1,0:T(8,128)(2,1)} %get-tuple-element.20) | copy-start | bytes 1622020
  94.3 4.2 %copy-start.5 = (bf16[24,2048]{1,0:T(8,128)(2,1)S(1)}, bf16[24,2048]{1,0:T(8,128)(2,1)}, u32[]{:S(2)}) copy-start(bf16[24,2048]{1,0:T(8,128)(2,1)} %get-tuple-element.40) | copy-start | bytes 294916
  94.3 4.8 %copy-start.4 = (bf16[24,2048]{1,0:T(8,128)(2,1)S(1)}, bf16[24,2048]{1,0:T(8,128)(2,1)}, u32[]{:S(2)}) copy-start(bf16[24,2048]{1,0:T(8,128)(2,1)} %get-tuple-element.41) | copy-start | bytes 294916

commit v2 on v1

--- a/solution.py
+++ b/solution.py
@@ -377,13 +377,20 @@
 
 
 def layer_kernel(depth, group, top, *refs):
-    ins, (wg_hbm, wu_hbm, wd_hbm) = refs[:3], refs[3:6]
+    (routes, route_gates, tokens, cotangent, wg_hbm, wu_hbm, wd_hbm), refs = refs[:7], refs[1:]
     (mixed, token_grad, gate_grad, row_tok, row_back, hid_t, pre_t, upv_t) = refs[6:14]
     (wg, wu, wd, row_rt, row_cot, tabs, row_gate, gp, up, bh, hid, pre, upv, ext_part, out_part, back_part, acc, gate_cols) = refs[14:32]
     dense, routed = refs[32:41], refs[41:46]
     weight_sem, own_sem, send_sem, recv_sem = refs[-4:]
-    bufs = refs[46:-4]
+    rt, square = refs[-6:-4]
+    bufs = refs[46:-6]
+    ins = (rt, tokens, cotangent)
     net = Net(depth, group, send_sem, recv_sem)
+    count = rt.shape[0]
+    square[...] = jnp.zeros_like(square)
+    square[:top, :count] = routes[...].astype(jnp.float32)
+    square[top : 2 * top, :count] = route_gates[...].astype(jnp.float32)
+    rt[...] = square[...].T[:count].astype(jnp.bfloat16)
     step = Dispatch(net, top, ins, (row_rt, row_tok, row_cot), tabs, dense, routed, own_sem)
     jobs = make_jobs(net, depth, group, tabs, (ext_part, out_part, back_part), (gate_cols, mixed, token_grad), bufs)
     forward, back = jobs[:3], jobs[3:]
@@ -496,21 +503,21 @@
         job.hop3()
     for job in forward:
         job.home()
-    count = gate_cols.shape[0]
     lane = lax.broadcasted_iota(jnp.int32, (count, LANES), 1)
     cols = gate_cols[...] + pltpu.roll(gate_cols[...], LANES // 2, 1)
-    routing = dense[0][net.z].astype(jnp.float32)
+    routing = rt[...].astype(jnp.float32)
     grads = jnp.zeros((count, LANES), jnp.float32)
     for k in range(top):
         hit = (routing[:, k : k + 1] == lane.astype(jnp.float32)) & (lane < LANES // 2)
         grads = jnp.where(lane == k, jnp.sum(jnp.where(hit, cols, 0.0), axis=1, keepdims=True), grads)
-    gate_grad[...] = grads
+    square[:count, :] = grads
+    gate_grad[...] = square[...].T[: gate_grad.shape[0]]
     for job in back:
         job.home()
     net.finish()
 
 
-def layer(experts, group, top, capacity, routing, tokens, cotangent, w_gate, w_up, w_down):
+def layer(experts, group, top, capacity, routes, route_gates, tokens, cotangent, w_gate, w_up, w_down):
     depth = experts // 4
     count, width = tokens.shape
     ff = w_gate.shape[1]
@@ -534,21 +541,53 @@
         out_shape=[
             jax.ShapeDtypeStruct((count, width), bf16),
             jax.ShapeDtypeStruct((count, width), bf16),
-            jax.ShapeDtypeStruct((count, LANES), f32),
+            jax.ShapeDtypeStruct((8, LANES), f32),
             jax.ShapeDtypeStruct(blocks + (width,), bf16),
             jax.ShapeDtypeStruct(blocks + (width,), bf16),
         ] + [jax.ShapeDtypeStruct((ff, slots), bf16)] * 3,
-        in_specs=[ANY_SPEC] * 6,
+        in_specs=[VMEM_SPEC] * 2 + [ANY_SPEC] * 5,
         out_specs=[VMEM_SPEC] * 8,
         scratch_shapes=scratch
         + dispatch_scratch(depth, count, span, width)
         + jobs_scratch(depth, group, count, span, width)
+        + [pltpu.VMEM((count, LANES), bf16), pltpu.VMEM((LANES, LANES), f32)]
         + [pltpu.SemaphoreType.DMA((3,)), pltpu.SemaphoreType.DMA((3,))]
         + semaphores(copies),
         compiler_params=pltpu.CompilerParams(
             collective_id=2, has_side_effects=True, vmem_limit_bytes=VMEM_LIMIT
         ),
-    )(routing, tokens, cotangent, w_gate, w_up, w_down)
+    )(routes.T, route_gates.T, tokens, cotangent, w_gate, w_up, w_down)
+
+
+def weight_kernel(hid_t, pre_t, upv_t, rows_in, rows_back, mixed_in, token_in, route_in, down, gate, up, mixed, token_grad, route_grad):
+    down[0] = dot_f32(hid_t[...], rows_back[...])
+    gate[0] = dot_f32(pre_t[...], rows_in[...])
+    up[0] = dot_f32(upv_t[...], rows_in[...])
+    mixed[...] = mixed_in[...]
+    token_grad[...] = token_in[...]
+    route_grad[...] = route_in[: route_grad.shape[0], : route_grad.shape[1]]
+
+
+def weight_grads(top, hid_t, pre_t, upv_t, rows_in, rows_back, mixed, token_grad, route_grad):
+    ff, slots = hid_t.shape
+    count, width = mixed.shape
+    chunk = 256
+    whole = lambda array: pl.BlockSpec(array.shape, lambda i: (0, 0))
+    columns = lambda array: pl.BlockSpec((array.shape[0], chunk), lambda i: (0, i))
+    wide = pl.BlockSpec((1, ff, chunk), lambda i: (0, 0, i))
+    grads = jax.ShapeDtypeStruct((1, ff, width), jnp.float32)
+    route = jax.ShapeDtypeStruct((top, count), jnp.float32)
+    return pl.pallas_call(
+        weight_kernel,
+        grid=(width // chunk,),
+        out_shape=[grads, grads, grads, mixed, token_grad, route],
+        in_specs=[whole(hid_t)] * 3 + [columns(rows_in)] * 2 + [columns(mixed)] * 2 + [whole(route_grad)],
+        out_specs=[wide] * 3 + [columns(mixed)] * 2 + [whole(route)],
+        cost_estimate=pl.CostEstimate(
+            flops=6 * slots * ff * width, bytes_accessed=12 * ff * width, transcendentals=0
+        ),
+        compiler_params=pltpu.CompilerParams(vmem_limit_bytes=VMEM_LIMIT),
+    )(hid_t, pre_t, upv_t, rows_in, rows_back, mixed, token_grad, route_grad)
 
 
 def per_device(tokens, cotangent, route_gates, routes, w_gate, w_up, w_down):
@@ -560,17 +599,17 @@
     gate_shard, up_shard, down_shard = (w_gate[0], w_up[0], w_down[0])
     me = lax.axis_index("expert")
 
+    if 2 * slots * width * tokens.dtype.itemsize <= FUSED_LIMIT:
+        mixed, token_grad, gate_grad, rows_in, rows_back, hid_t, pre_t, upv_t = layer(
+            experts, group, top_count, capacity, routes, route_gates, tokens, cotangent, w_gate, w_up, w_down
+        )
+        rows_in, rows_back = rows_in.reshape(slots, width), rows_back.reshape(slots, width)
+        grad_down, grad_gate, grad_up, mixed, token_grad, gate_grad = weight_grads(
+            top_count, hid_t, pre_t, upv_t, rows_in, rows_back, mixed, token_grad, gate_grad
+        )
+        return (mixed, token_grad, gate_grad.T, grad_gate, grad_up, grad_down)
     routing = jnp.concatenate([routes.astype(jnp.bfloat16), route_gates], axis=1)
     routing = jnp.pad(routing, ((0, 0), (0, LANES - 2 * top_count)))
-    if 2 * slots * width * tokens.dtype.itemsize <= FUSED_LIMIT:
-        mixed, token_grad, gate_grad, rows_in, rows_back, hid_t, pre_t, upv_t = layer(
-            experts, group, top_count, capacity, routing, tokens, cotangent, w_gate, w_up, w_down
-        )
-        rows_in, rows_back = rows_in.reshape(slots, width), rows_back.reshape(slots, width)
-        grad_down = dot_f32(hid_t, rows_back)
-        grad_gate = dot_f32(pre_t, rows_in)
-        grad_up = dot_f32(upv_t, rows_in)
-        return (mixed, token_grad, gate_grad[:, :top_count], grad_gate[None], grad_up[None], grad_down[None])
     row_rt, row_tok, row_cot, tabs = dispatch(experts, group, top_count, capacity, routing, tokens, cotangent)
     shape = row_tok.shape
     row_rt = row_rt.reshape(slots, LANES).astype(jnp.float32)

time: 100 us -> 92.5 us (0.925)
  matrix products: 14.3 us -> 0 us
  Pallas kernels: 79.9 us -> 91.5 us
  local copies, waits for them, and re-layouts: 3.55 us -> 0 us
  other arithmetic: 1.37 us -> 0 us
    dot_general x3 -> x0, matrix products: 14.3 us -> none  [dot_f32(): lax.dot_general(left, right, dims, preferred_element_type=jnp.float32)]
    pallas_call x0 -> x1, Pallas kernels: none -> 11.6 us  [weight_grads(): pl.pallas_call(weight_kernel, grid=(width // chunk,), out_shape=[grads, g...]
    unnamed x16 -> x0, local copies, waits for them, and re-layouts: 3.45 us -> none
where the time goes in v2:
time: 92.5 us; the launch traced here: 92.1 us
  Pallas kernels  91.5 us (99%)
    pallas_call x1, Pallas kernels, layer(): pl.pallas_call(functools.partial(layer_kernel, depth, group, top), out_sh...  79.9 us
    pallas_call x1, Pallas kernels, weight_grads(): pl.pallas_call(weight_kernel, grid=(width // chunk,), out_shape=[grads, g...  11.6 us

profile of v2, /device:TPU:0, one launch (start us, length us, event | category | flops | bytes accessed | tf_op | source)
XLA Modules:
  0.0 92.1 jit_solution(14859493550557049494)
XLA Ops:
  0.6 79.9 %shard_map.118 = (bf16[24,2048]{1,0:T(8,128)(2,1)}, bf16[24,2048]{1,0:T(8,128)(2,1)}, f32[8,128]{1,0:T(8,128)}, bf16[2,2,2,48,2048]{4,3,2,1,0:T(8,128)(2,1)}, bf...) custom-call(s32[6,24]{1,0:T(8,128)} %bitcast.5, ...), custom_call_target="tpu_custom_call" | custom-call | tf_op jit(solution)/shard_map/pallas_call | solution.py:539
  80.5 11.6 %shard_map.119 = (f32[1,704,2048]{2,1,0:T(8,128)}, f32[1,704,2048]{2,1,0:T(8,128)}, f32[1,704,2048]{2,1,0:T(8,128)}, bf16[24,2048]{1,0:T(8,128)(2,1)}, bf16[24,2048]{1,0:T(8,128)(2,1)}, /*index=5*/f32[6,24]{1,0:T(8,128)}) custom-call(bf16[704,384]{1,0:T(8,128)(2,1)} %get-tuple-element.20.hid_t, bf16[704,384]{1,0:T(8,128)(2,1)} %get-tuple-element.21.pre_t, ...), custom_call_target="tpu_custom_call" | custom-call | flops 3321888768 | bytes 17301504 | tf_op jit(solution)/shard_map/pallas_call | solution.py:580

commit v3 on v2

--- a/solution.py
+++ b/solution.py
@@ -12,6 +12,8 @@
 LANES = 128
 VMEM_LIMIT = 60 * 1024 * 1024
 FUSED_LIMIT = 4 * 1024 * 1024
+PARTS = 4
+ORDER = (0, 2, 1, 3)
 
 
 def dot_f32(left, right, dims=(((1,), (0,)), ((), ()))):
@@ -72,12 +74,17 @@
         self.near, self.up, self.by = dense[:3], dense[3:6], dense[6:9]
         self.send0, self.send1 = (routed[0], routed[1], routed[2]), (None, routed[3], routed[4])
         self.own_sem = own_sem
-        half = ins[1].shape[1] // 2
-        self.low = (pl.ds(0, LANES), pl.ds(0, half), pl.ds(0, half))
-        self.high = pl.ds(half, half)
+        self.half, self.chunk = ins[1].shape[1] // 2, ins[1].shape[1] // PARTS
         self.span = rows[0].shape[3]
-        self.pending = []
-        self.moved0, self.moved1, self.deep, self.side0, self.side1 = {}, {}, {}, {}, {}
+        self.units = [(t, c) for t in (1, 2) for c in ORDER]
+        self.pending, self.moved, self.deep, self.side = {}, {}, {}, {}
+
+    def cols(self, unit):
+        t, c = unit
+        if t == 0:
+            return 0, pl.ds(0, LANES), pl.ds(0, LANES)
+        kind = int(2 * c >= PARTS)
+        return kind, pl.ds(c * self.chunk, self.chunk), pl.ds(c * self.chunk - kind * self.half, self.chunk)
 
     def start(self):
         net = self.net
@@ -86,29 +93,28 @@
             copy = pltpu.make_async_copy(self.ins[t], self.near[t].at[net.z], self.own_sem.at[t])
             copy.start()
             own.append(copy)
-        self.push_deep(0)
-        self.push_deep(1)
+        for unit in [(0, 0)] + self.units:
+            t, (_, wide, _) = unit[0], self.cols(unit)
+            self.deep[unit] = [net.push(self.ins[t].at[:, wide], self.near[t].at[net.z, :, wide], peer) for peer in net.deep]
         for copy in own:
             copy.wait()
 
-    def push_deep(self, t):
-        net = self.net
-        self.deep[t] = [net.push(self.ins[t], self.near[t].at[net.z], peer) for peer in net.deep]
-
-    def push_side(self, t):
-        net = self.net
-        arrived(self.deep[t])
+    def push_side(self, unit):
+        net, t = self.net, unit[0]
+        kind, wide, thin = self.cols(unit)
+        arrived(self.deep[unit])
         if t == 0:
-            self.side0[t] = net.push(self.near[t], self.up[t], net.across)
-            self.side1[t] = net.push(self.near[t], self.by[t], net.beside)
+            self.side[unit] = net.push(self.near[t], self.up[t], net.across)
+            self.side_by = net.push(self.near[t], self.by[t], net.beside)
+        elif kind == 0:
+            self.side[unit] = net.push(self.near[t].at[:, :, wide], self.up[t].at[:, :, thin], net.across)
         else:
-            self.side0[t] = net.push(self.near[t].at[:, :, self.low[t]], self.up[t], net.across)
-            self.side1[t] = net.push(self.near[t].at[:, :, self.high], self.by[t], net.beside)
+            self.side[unit] = net.push(self.near[t].at[:, :, wide], self.by[t].at[:, :, thin], net.beside)
 
     def tables(self):
         net, span, count = self.net, self.span, self.ins[0].shape[0]
-        self.side0[0].wait_recv()
-        self.side1[0].wait_recv()
+        self.side[0, 0].wait_recv()
+        self.side_by.wait_recv()
         depth = self.near[0].shape[0]
         total = depth * count
         lane = lax.broadcasted_iota(jnp.int32, (total, LANES), 1)
@@ -145,38 +151,61 @@
         rows = dot_f32(self.tabs[which, 0], flat(near), OUTER) + dot_f32(self.tabs[which, 1], flat(far), OUTER)
         return rows[: 2 * self.span].astype(jnp.bfloat16).reshape(2, self.span, -1)
 
-    def share(self, view):
-        self.pending += [self.net.push(view, view, peer) for peer in self.net.mates]
-
-    def first_way(self, t):
-        net, cols, send, rows = self.net, self.low[t], self.send0[t], self.rows[t]
-        self.side0[t].wait_recv() if t else None
-        near, far = self.near[t][:, :, cols], self.up[t][...]
-        send[...] = self.chosen(1, near, far)
-        self.moved0[t] = net.push(send, rows.at[net.core, net.x, :, :, cols], net.beside)
-        rows[net.core, net.x, :, :, cols] = self.chosen(0, near, far)
-        self.share(rows.at[net.core, net.x, :, :, cols])
-
-    def second_way(self, t):
-        net, cols, send, rows = self.net, self.high, self.send1[t], self.rows[t]
-        self.side1[t].wait_recv()
-        near, far = self.near[t][:, :, cols], self.by[t][...]
-        send[...] = self.chosen(3, near, far)
-        self.moved1[t] = net.push(send, rows.at[net.core, :, net.y, :, cols], net.across)
-        rows[net.core, :, net.y, :, cols] = self.chosen(2, near, far)
-        self.share(rows.at[net.core, :, net.y, :, cols])
-
-    def last(self, t):
-        net, rows = self.net, self.rows[t]
-        self.moved0[t].wait_recv()
-        self.share(rows.at[net.core, 1 - net.x, :, :, self.low[t]])
+    def share(self, unit, view):
+        self.pending.setdefault(unit, []).extend([self.net.push(view, view, peer) for peer in self.net.mates])
+
+    def route(self, unit):
+        net, t = self.net, unit[0]
+        kind, wide, thin = self.cols(unit)
+        rows, send, other = self.rows[t], (self.send0, self.send1)[kind][t], (self.up, self.by)[kind][t]
         if t:
-            self.moved1[t].wait_recv()
-            self.share(rows.at[net.core, :, 1 - net.y, :, self.high])
-
-    def settle(self):
-        arrived(self.pending)
-        self.pending = []
+            self.side[unit].wait_recv()
+        near, far = self.near[t][:, :, wide], other[:, :, thin]
+        send[:, :, thin] = self.chosen(1 + 2 * kind, near, far)
+        target = rows.at[net.core, net.x, :, :, wide] if kind == 0 else rows.at[net.core, :, net.y, :, wide]
+        self.moved[unit] = net.push(send.at[:, :, thin], target, (net.beside, net.across)[kind])
+        target[...] = self.chosen(2 * kind, near, far)
+        self.share(unit, target)
+
+    def last(self, unit):
+        net, rows = self.net, self.rows[unit[0]]
+        kind, wide, _ = self.cols(unit)
+        self.moved[unit].wait_recv()
+        if kind == 0:
+            self.share(unit, rows.at[net.core, 1 - net.x, :, :, wide])
+        else:
+            self.share(unit, rows.at[net.core, :, 1 - net.y, :, wide])
+
+    def settle(self, units):
+        for unit in units:
+            arrived(self.pending[unit])
+
+    def first_half(self):
+        u, rt = self.units, (0, 0)
+        self.start()
+        self.push_side(rt)
+        self.push_side(u[0])
+        self.tables()
+        self.route(rt)
+        self.push_side(u[1])
+        self.route(u[0])
+        self.push_side(u[2])
+        self.route(u[1])
+        self.push_side(u[3])
+        self.last(rt)
+        self.last(u[0])
+        self.route(u[2])
+        self.push_side(u[4])
+        self.last(u[1])
+        self.route(u[3])
+        self.push_side(u[5])
+        self.last(u[2])
+        self.route(u[4])
+        self.push_side(u[6])
+        self.last(u[3])
+        self.route(u[5])
+        self.push_side(u[7])
+        self.settle([rt] + u[:4])
 
 
 def dispatch_kernel(depth, group, top, *refs):
@@ -185,21 +214,13 @@
     net = Net(depth, group, send_sem, recv_sem)
     step = Dispatch(net, top, ins, rows, tabs, refs[7:16], refs[16:21], own_sem)
     net.barrier()
-    step.start()
-    step.push_side(0)
-    step.push_side(1)
-    step.push_deep(2)
-    step.tables()
-    step.first_way(0)
-    step.first_way(1)
-    step.second_way(1)
-    step.push_side(2)
-    step.last(0)
-    step.last(1)
-    step.first_way(2)
-    step.second_way(2)
-    step.last(2)
-    step.settle()
+    step.first_half()
+    u = step.units
+    for unit in u[6:]:
+        step.route(unit)
+    for unit in u[4:]:
+        step.last(unit)
+    step.settle(u[4:])
     net.finish()
 
 
@@ -210,7 +231,7 @@
 
 
 def dispatch_copies(depth, group):
-    return 3 * (depth - 1) + 6 + 5 + 10 * (group - 1)
+    return (2 * PARTS + 1) * (depth + 1 + 2 * (group - 1)) + 1
 
 
 def semaphores(copies):
@@ -245,16 +266,17 @@
     )(routing, tokens, cotangent)
 
 
-JOBS = ((0, 0), (1, 0), (1, 1), (2, 0), (2, 1))
+JOBS = ((0, 0),) + tuple((source, c) for source in (1, 2) for c in ORDER)
 
 
 class Job:
-    def __init__(self, net, depth, group, tabs, part, out, kind, bufs):
+    def __init__(self, net, depth, group, tabs, part, out, place, bufs):
+        kind = int(2 * place >= PARTS)
         self.net, self.depth, self.group, self.tabs = net, depth, group, tabs
         self.part, self.out, self.kind = part, out, kind
         (self.mate, self.give, self.own, self.take, self.far, self.near, self.came, self.deep) = bufs
         width = self.give.shape[-1]
-        self.cols, self.every = pl.ds(kind * width, width), pl.ds(0, width)
+        self.cols, self.every = pl.ds(place * width, width), pl.ds(0, width)
         self.first, self.second = (net.beside, net.across) if kind == 0 else (net.across, net.beside)
 
     def pick(self, ref, lead, remote, cols):
@@ -324,9 +346,9 @@
 
 
 def jobs_scratch(depth, group, count, span, width):
-    bf16, half, bufs = jnp.bfloat16, width // 2, []
-    for source, kind in JOBS:
-        w = LANES if source == 0 else half
+    bf16, chunk, bufs = jnp.bfloat16, width // PARTS, []
+    for source, _ in JOBS:
+        w = LANES if source == 0 else chunk
         bufs += [pltpu.VMEM((max(1, group - 1), 2, 2, span, w), bf16)]
         bufs += [pltpu.VMEM((2, span, w), bf16)] * 3
         bufs += [pltpu.VMEM((depth, count, w), bf16)] * 4
@@ -339,8 +361,8 @@
 
 def make_jobs(net, depth, group, tabs, parts, outs, bufs):
     return [
-        Job(net, depth, group, tabs, parts[source], outs[source], kind, bufs[8 * i : 8 * i + 8])
-        for i, (source, kind) in enumerate(JOBS)
+        Job(net, depth, group, tabs, parts[source], outs[source], place, bufs[8 * i : 8 * i + 8])
+        for i, (source, place) in enumerate(JOBS)
     ]
 
 
@@ -393,30 +415,20 @@
     rt[...] = square[...].T[:count].astype(jnp.bfloat16)
     step = Dispatch(net, top, ins, (row_rt, row_tok, row_cot), tabs, dense, routed, own_sem)
     jobs = make_jobs(net, depth, group, tabs, (ext_part, out_part, back_part), (gate_cols, mixed, token_grad), bufs)
-    forward, back = jobs[:3], jobs[3:]
+    ext, forward, back = jobs[0], jobs[1 : 1 + PARTS], jobs[1 + PARTS :]
     slots, ff, width = gp.shape[0], wg.shape[0], wg.shape[1]
     lead = row_tok.shape[:4]
-    chunk = 512
+    chunk = width // PARTS
     net.barrier()
     weights = []
     for i, (src, dst) in enumerate(((wg_hbm, wg), (wu_hbm, wu), (wd_hbm, wd))):
         copy = pltpu.make_async_copy(src.at[0], dst, weight_sem.at[i])
         weights.append(copy)
 
-    step.start()
     for copy in weights:
         copy.start()
-    step.push_side(0)
-    step.push_side(1)
-    step.push_deep(2)
-    step.tables()
-    step.first_way(0)
-    step.first_way(1)
-    step.second_way(1)
-    step.push_side(2)
-    step.last(0)
-    step.last(1)
-    step.settle()
+    step.first_half()
+    units = step.units
 
     lane = lax.broadcasted_iota(jnp.int32, (slots, LANES), 1)
     routing = row_rt[...].reshape(slots, LANES).astype(jnp.float32)
@@ -427,10 +439,11 @@
     for copy in weights:
         copy.wait()
     gp[...] = dot_f32(row_tok[...].reshape(slots, width), wg[...], INNER)
-    step.first_way(2)
-    step.second_way(2)
+    step.last(units[4])
+    step.route(units[6])
     up[...] = dot_f32(row_tok[...].reshape(slots, width), wu[...], INNER)
-    step.last(2)
+    step.route(units[7])
+    step.last(units[5])
 
     rows = 16
 
@@ -440,32 +453,50 @@
         g = gp[at, :]
         hid[at, pl.ds(0, ff)] = (g * jax.nn.sigmoid(g) * up[at, :]).astype(jnp.bfloat16)
 
-    step.settle()
+    step.last(units[6])
+    step.last(units[7])
+    step.settle(units[4:])
     acc[...] = jnp.zeros_like(acc)
 
-    @pl.loop(0, width // chunk)
-    def _(i):
-        cols = pl.ds(pl.multiple_of(i * chunk, chunk), chunk)
+    def out_cols(job):
+        cols = job.cols
         value = dot_f32(hid[:, :ff], wd[:, cols])
         cot = row_cot[:, :, :, :, cols].reshape(slots, chunk).astype(jnp.float32)
         product = value * cot
+        total = acc[...]
         for j in range(chunk // LANES):
-            acc[...] += product[:, j * LANES : (j + 1) * LANES]
+            total = total + product[:, j * LANES : (j + 1) * LANES]
+        acc[...] = total
         gate = row_gate[:, :1]
         out_part[:, :, :, :, cols] = (value * gate).astype(jnp.bfloat16).reshape(lead + (chunk,))
         row_back[:, :, :, :, cols] = (cot * gate).astype(jnp.bfloat16).reshape(lead + (chunk,))
+        job.exchange()
+
+    f = forward
+    out_cols(f[0])
+    out_cols(f[1])
+    f[0].hop1()
+    out_cols(f[2])
+    f[1].hop1()
+    out_cols(f[3])
+    f[2].hop1()
+    f[0].keep()
+    f[1].keep()
 
     row_grad = jnp.sum(acc[...], axis=1, keepdims=True)
     row_high = row_grad.astype(jnp.bfloat16).astype(jnp.float32)
     row_low = row_grad - row_high
-    ext = jnp.where(lane == net.me, row_high, jnp.where(lane == LANES // 2 + net.me, row_low, 0.0))
-    ext_part[...] = ext.astype(jnp.bfloat16).reshape(ext_part.shape)
-    for job in forward:
-        job.exchange()
+    columns = jnp.where(lane == net.me, row_high, jnp.where(lane == LANES // 2 + net.me, row_low, 0.0))
+    ext_part[...] = columns.astype(jnp.bfloat16).reshape(ext_part.shape)
+    ext.exchange()
     bh[...] = dot_f32(row_back[...].reshape(slots, width), wd[...], INNER)
-    for name in ("hop1", "keep"):
-        for job in forward:
-            getattr(job, name)()
+    f[3].hop1()
+    ext.hop1()
+    f[2].keep()
+    f[3].keep()
+    ext.keep()
+    f[0].hop2()
+    f[1].hop2()
 
     @pl.loop(0, slots // rows)
     def _(i):
@@ -475,33 +506,45 @@
         pre[at, pl.ds(0, ff)] = (b * up[at, :] * s * (1.0 + g * (1.0 - s))).astype(jnp.bfloat16)
         upv[at, pl.ds(0, ff)] = (b * g * s).astype(jnp.bfloat16)
 
-    def back_cols(first, last):
-        @pl.loop(first, last)
-        def _(i):
-            cols = pl.ds(pl.multiple_of(i * chunk, chunk), chunk)
-            value = dot_f32(pre[:, :ff], wg[:, cols]) + dot_f32(upv[:, :ff], wu[:, cols])
-            back_part[:, :, :, :, cols] = value.astype(jnp.bfloat16).reshape(lead + (chunk,))
-
-    for job in forward:
-        job.hop2()
-    middle = width // chunk // 2
-    back_cols(0, middle)
-    back[0].exchange()
-    back_cols(middle, 2 * middle)
-    back[1].exchange()
-    for job in forward:
-        job.hop3()
-    for job in back:
-        job.hop1()
-    for job in back:
-        job.keep()
+    f[2].hop2()
+    f[3].hop2()
+    ext.hop2()
+
+    def back_cols(job):
+        cols = job.cols
+        value = dot_f32(pre[:, :ff], wg[:, cols]) + dot_f32(upv[:, :ff], wu[:, cols])
+        back_part[:, :, :, :, cols] = value.astype(jnp.bfloat16).reshape(lead + (chunk,))
+        job.exchange()
+
+    b = back
+    back_cols(b[0])
+    f[0].hop3()
+    back_cols(b[1])
+    b[0].hop1()
+    f[1].hop3()
+    b[0].keep()
+    back_cols(b[2])
+    b[1].hop1()
+    f[2].hop3()
+    b[1].keep()
+    back_cols(b[3])
+    b[2].hop1()
+    f[3].hop3()
+    ext.hop3()
+    b[2].keep()
+    b[0].hop2()
+    b[3].hop1()
+    b[3].keep()
+    b[1].hop2()
+    b[2].hop2()
+    b[0].hop3()
+    b[3].hop2()
+    b[1].hop3()
+    b[2].hop3()
+    b[3].hop3()
     for src, dst in ((hid, hid_t), (pre, pre_t), (upv, upv_t)):
         dst[...] = src[...].T[:ff]
-    for job in back:
-        job.hop2()
-    for job in back:
-        job.hop3()
-    for job in forward:
+    for job in [ext] + forward:
         job.home()
     lane = lax.broadcasted_iota(jnp.int32, (count, LANES), 1)
     cols = gate_cols[...] + pltpu.roll(gate_cols[...], LANES // 2, 1)

time: 92.5 us -> 89.7 us (0.970)
  Pallas kernels: 91.5 us -> 88.5 us
    pallas_call x1, Pallas kernels: 79.9 us -> 76.9 us  [layer(): pl.pallas_call(functools.partial(layer_kernel, depth, group, top), out_sh...]
where the time goes in v3:
time: 89.7 us; the launch traced here: 89.3 us
  Pallas kernels  88.5 us (99%)
    pallas_call x1, Pallas kernels, layer(): pl.pallas_call(functools.partial(layer_kernel, depth, group, top), out_sh...  76.9 us
    pallas_call x1, Pallas kernels, weight_grads(): pl.pallas_call(weight_kernel, grid=(width // chunk,), out_shape=[grads, g...  11.6 us

profile of v3, /device:TPU:0, one launch (start us, length us, event | category | flops | bytes accessed | tf_op | source)
XLA Modules:
  0.0 89.3 jit_solution(4066089056956941141)
XLA Ops:
  0.6 76.9 %shard_map.118 = (bf16[24,2048]{1,0:T(8,128)(2,1)}, bf16[24,2048]{1,0:T(8,128)(2,1)}, f32[8,128]{1,0:T(8,128)}, bf16[2,2,2,48,2048]{4,3,2,1,0:T(8,128)(2,1)}, bf...) custom-call(s32[6,24]{1,0:T(8,128)} %bitcast.5, ...), custom_call_target="tpu_custom_call" | custom-call | tf_op jit(solution)/shard_map/pallas_call | solution.py:582
  77.6 11.6 %shard_map.119 = (f32[1,704,2048]{2,1,0:T(8,128)}, f32[1,704,2048]{2,1,0:T(8,128)}, f32[1,704,2048]{2,1,0:T(8,128)}, bf16[24,2048]{1,0:T(8,128)(2,1)}, bf16[24,2048]{1,0:T(8,128)(2,1)}, /*index=5*/f32[6,24]{1,0:T(8,128)}) custom-call(bf16[704,384]{1,0:T(8,128)(2,1)} %get-tuple-element.20.hid_t, bf16[704,384]{1,0:T(8,128)(2,1)} %get-tuple-element.21.pre_t, ...), custom_call_target="tpu_custom_call" | custom-call | flops 3321888768 | bytes 17301504 | tf_op jit(solution)/shard_map/pallas_call | solution.py:623

commit v4 on v3

--- a/solution.py
+++ b/solution.py
@@ -35,6 +35,8 @@
         self.across_id, self.beside_id = self.across[0], self.beside[0]
         self.send_sem, self.recv_sem = send_sem, recv_sem
         self.sent, self.used = [], 0
+        self.depth, self.chain = depth, []
+        self.above, self.below = at((z + 1) % depth, y, x, core), at((z + depth - 1) % depth, y, x, core)
 
     def barrier(self):
         peers = self.deep + [self.across, self.beside] + self.mates
@@ -54,7 +56,20 @@
         self.sent.append(copy)
         return copy
 
+    def link(self, src, dst, peer, going, coming):
+        index = self.used
+        self.used += 1
+        copy = pltpu.make_async_remote_copy(
+            src_ref=src, dst_ref=dst, send_sem=self.send_sem.at[index], recv_sem=self.recv_sem.at[index],
+            device_id=peer, device_id_type=pl.DeviceIdType.MESH,
+        )
+        pl.when(going)(copy.start)
+        self.chain.append((going, copy))
+        return lambda: pl.when(coming)(copy.wait_recv)
+
     def finish(self):
+        for going, copy in self.chain:
+            pl.when(going)(copy.wait_send)
         for copy in self.sent:
             copy.wait_send()
 
@@ -93,16 +108,28 @@
             copy = pltpu.make_async_copy(self.ins[t], self.near[t].at[net.z], self.own_sem.at[t])
             copy.start()
             own.append(copy)
-        for unit in [(0, 0)] + self.units:
-            t, (_, wide, _) = unit[0], self.cols(unit)
-            self.deep[unit] = [net.push(self.ins[t].at[:, wide], self.near[t].at[net.z, :, wide], peer) for peer in net.deep]
         for copy in own:
             copy.wait()
+
+    def forward(self, unit, stage):
+        net, z, depth = self.net, self.net.z, self.net.depth
+        near, wide = self.near[unit[0]], self.cols(unit)[1]
+        if stage > 1:
+            for wait in self.deep[unit]:
+                wait()
+        up, down = z - stage + 1, z + stage - 1
+        low, high = jnp.maximum(up, 0), jnp.minimum(down, depth - 1)
+        rising, falling = near.at[low, :, wide], near.at[high, :, wide]
+        self.deep[unit] = [
+            net.link(rising, rising, net.above, (up >= 0) & (z + 1 < depth), z - stage >= 0),
+            net.link(falling, falling, net.below, (down < depth) & (z >= 1), z + stage < depth),
+        ]
 
     def push_side(self, unit):
         net, t = self.net, unit[0]
         kind, wide, thin = self.cols(unit)
-        arrived(self.deep[unit])
+        for wait in self.deep[unit]:
+            wait()
         if t == 0:
             self.side[unit] = net.push(self.near[t], self.up[t], net.across)
             self.side_by = net.push(self.near[t], self.by[t], net.beside)
@@ -182,29 +209,41 @@
 
     def first_half(self):
         u, rt = self.units, (0, 0)
+        early, late, depth = [rt] + u[:4], u[4:], self.net.depth
         self.start()
+        for unit in early:
+            self.forward(unit, 1)
+        for stage in range(2, depth + 1):
+            for unit in early if stage < depth else []:
+                self.forward(unit, stage)
+            for unit in late if stage < depth else []:
+                self.forward(unit, stage - 1)
         self.push_side(rt)
         self.push_side(u[0])
+        self.push_side(u[1])
+        for unit in late[:2]:
+            self.forward(unit, depth - 1)
         self.tables()
         self.route(rt)
-        self.push_side(u[1])
+        self.push_side(u[2])
+        self.push_side(u[3])
+        for unit in late[2:]:
+            self.forward(unit, depth - 1)
         self.route(u[0])
-        self.push_side(u[2])
         self.route(u[1])
-        self.push_side(u[3])
-        self.last(rt)
-        self.last(u[0])
         self.route(u[2])
         self.push_side(u[4])
+        self.route(u[3])
+        self.last(rt)
+        self.push_side(u[5])
+        self.last(u[0])
         self.last(u[1])
-        self.route(u[3])
-        self.push_side(u[5])
+        self.push_side(u[6])
+        self.push_side(u[7])
         self.last(u[2])
         self.route(u[4])
-        self.push_side(u[6])
         self.last(u[3])
         self.route(u[5])
-        self.push_side(u[7])
         self.settle([rt] + u[:4])
 
 
@@ -231,7 +270,7 @@
 
 
 def dispatch_copies(depth, group):
-    return (2 * PARTS + 1) * (depth + 1 + 2 * (group - 1)) + 1
+    return (2 * PARTS + 1) * (2 * depth + 2 * (group - 1)) + 1
 
 
 def semaphores(copies):
@@ -326,20 +365,47 @@
         self.near[...] = self.spread(0)
 
     def hop3(self):
-        net, depth = self.net, self.depth
         self.copy2.wait_recv()
         self.near[...] = (self.near[...].astype(jnp.float32) + self.came[...].astype(jnp.float32)).astype(jnp.bfloat16)
-        self.copies3 = [
-            net.push(self.near.at[(net.z + k) % depth], self.deep.at[net.z], net.deep[k - 1]) for k in range(1, depth)
-        ]
+        self.up_wait, self.down_wait = {}, {}
+
+    def add(self, block, side):
+        self.near[block] = (self.near[block].astype(jnp.float32) + self.deep[side, block].astype(jnp.float32)).astype(jnp.bfloat16)
+
+    def along(self, stage):
+        net, z, depth = self.net, self.net.z, self.depth
+        up, down = depth - 1 - stage, stage
+        for block, side, peer, passing, going, coming in (
+            (up, 0, net.above, (z > 0) & (z < up), z < up, (z > 0) & (z <= up)),
+            (down, 1, net.below, (z < depth - 1) & (z > down), z > down, (z < depth - 1) & (z >= down)),
+        ):
+            copy = pltpu.make_async_remote_copy(
+                src_ref=self.near.at[block], dst_ref=self.deep.at[side, block],
+                send_sem=net.send_sem.at[net.used], recv_sem=net.recv_sem.at[net.used],
+                device_id=peer, device_id_type=pl.DeviceIdType.MESH,
+            )
+            net.used += 1
+
+            @pl.when(passing)
+            def _():
+                copy.wait_recv()
+                self.add(block, side)
+
+            pl.when(going)(copy.start)
+            net.chain.append((going, copy))
+            (self.up_wait, self.down_wait)[side][block] = copy
 
     def sum(self):
         z, depth = self.net.z, self.depth
-        arrived(self.copies3)
-        acc = self.near[z].astype(jnp.float32)
-        for k in range(1, depth):
-            acc = acc + self.deep[(z + k) % depth].astype(jnp.float32)
-        return acc
+        for side, waits in ((0, self.up_wait), (1, self.down_wait)):
+            for block, copy in waits.items():
+
+                @pl.when(z == block)
+                def _():
+                    copy.wait_recv()
+                    self.add(block, side)
+
+        return self.near[z].astype(jnp.float32)
 
     def home(self):
         self.out[:, self.cols] = self.sum().astype(self.out.dtype)
@@ -351,12 +417,13 @@
         w = LANES if source == 0 else chunk
         bufs += [pltpu.VMEM((max(1, group - 1), 2, 2, span, w), bf16)]
         bufs += [pltpu.VMEM((2, span, w), bf16)] * 3
-        bufs += [pltpu.VMEM((depth, count, w), bf16)] * 4
+        bufs += [pltpu.VMEM((depth, count, w), bf16)] * 3
+        bufs += [pltpu.VMEM((2, depth, count, w), bf16)]
     return bufs
 
 
 def jobs_copies(depth, group):
-    return len(JOBS) * (2 * (group - 1) + 2 + depth - 1)
+    return len(JOBS) * (2 * (group - 1) + 2 * depth)
 
 
 def make_jobs(net, depth, group, tabs, parts, outs, bufs):
@@ -371,9 +438,14 @@
     net = Net(depth, group, refs[-2], refs[-1])
     net.barrier()
     jobs = make_jobs(net, depth, group, tabs, parts, outs, refs[7:-2])
-    for name in ("exchange", "hop1", "keep", "hop2", "hop3", "home"):
+    for name in ("exchange", "hop1", "keep", "hop2", "hop3"):
         for job in jobs:
             getattr(job, name)()
+    for stage in range(depth - 1):
+        for job in jobs:
+            job.along(stage)
+    for job in jobs:
+        job.home()
     net.finish()
 
 
@@ -532,16 +604,23 @@
     f[3].hop3()
     ext.hop3()
     b[2].keep()
-    b[0].hop2()
+    for job in [ext] + f:
+        job.along(0)
     b[3].hop1()
     b[3].keep()
+    b[0].hop2()
     b[1].hop2()
+    for stage in range(1, depth - 1):
+        for job in [ext] + f:
+            job.along(stage)
     b[2].hop2()
-    b[0].hop3()
     b[3].hop2()
-    b[1].hop3()
-    b[2].hop3()
-    b[3].hop3()
+    for job in b:
+        job.hop3()
+        job.along(0)
+    for stage in range(1, depth - 1):
+        for job in b:
+            job.along(stage)
     for src, dst in ((hid, hid_t), (pre, pre_t), (upv, upv_t)):
         dst[...] = src[...].T[:ff]
     for job in [ext] + forward:

time: 89.7 us -> 140 us (1.56)
  Pallas kernels: 88.5 us -> 139 us
    pallas_call x1, Pallas kernels: 76.9 us -> 127 us  [layer(): pl.pallas_call(functools.partial(layer_kernel, depth, group, top), out_sh...]
where the time goes in v4:
time: 140 us; the launch traced here: 139 us
  Pallas kernels  139 us (99%)
    pallas_call x1, Pallas kernels, layer(): pl.pallas_call(functools.partial(layer_kernel, depth, group, top), out_sh...  127 us
    pallas_call x1, Pallas kernels, weight_grads(): pl.pallas_call(weight_kernel, grid=(width // chunk,), out_shape=[grads, g...  11.6 us

profile of v4, /device:TPU:0, one launch (start us, length us, event | category | flops | bytes accessed | tf_op | source)
XLA Modules:
  0.0 139.4 jit_solution(18190764587265510868)
XLA Ops:
  0.6 127.0 %shard_map.118 = (bf16[24,2048]{1,0:T(8,128)(2,1)}, bf16[24,2048]{1,0:T(8,128)(2,1)}, f32[8,128]{1,0:T(8,128)}, bf16[2,2,2,48,2048]{4,3,2,1,0:T(8,128)(2,1)}, bf...) custom-call(s32[6,24]{1,0:T(8,128)} %bitcast.5, ...), custom_call_target="tpu_custom_call" | custom-call | tf_op jit(solution)/shard_map/pallas_call | solution.py:661
  127.7 11.6 %shard_map.119 = (f32[1,704,2048]{2,1,0:T(8,128)}, f32[1,704,2048]{2,1,0:T(8,128)}, f32[1,704,2048]{2,1,0:T(8,128)}, bf16[24,2048]{1,0:T(8,128)(2,1)}, bf16[24,2048]{1,0:T(8,128)(2,1)}, /*index=5*/f32[6,24]{1,0:T(8,128)}) custom-call(bf16[704,384]{1,0:T(8,128)(2,1)} %get-tuple-element.20.hid_t, bf16[704,384]{1,0:T(8,128)(2,1)} %get-tuple-element.21.pre_t, ...), custom_call_target="tpu_custom_call" | custom-call | flops 3321888768 | bytes 17301504 | tf_op jit(solution)/shard_map/pallas_call | solution.py:702
